TPU v7x, 256 devices: a whole 4x4x8 slice. The times are simulated.
256 devices in a mesh: ctx: 8 (over x, y_lo), mp: 32 (over z, y_hi, core).
Axes of the slice: x: 4, y: 4 (y_hi: 2, y_lo: 2; y = y_hi * 2 + y_lo), z: 8, core: 2. Of those that a mesh axis runs over, the one named last changes fastest.
Arguments:
- residual_in: bfloat16 [4096, 8192], P('ctx', 'mp'), may hold values from -4 to 4
- query_rows: bfloat16 [4096, 8192], P('ctx', 'mp'), may hold values from -5 to 5
- key_rows: bfloat16 [4096, 8192], P('ctx', 'mp'), may hold values from -5 to 5
- value_rows: bfloat16 [4096, 8192], P('ctx', 'mp'), may hold values from -5 to 5
- out_weight: bfloat16 [8192, 8192], P('mp'), may hold values from -1 to 1
- gate_in: bfloat16 [4096, 8192], P('ctx', 'mp'), may hold values from -5 to 5
- gate_out: bfloat16 [4096, 8192], P('ctx', 'mp'), may hold values from -5 to 5
- short_taps: float32 [3, 8192], P(None, 'mp'), may hold values from -3 to 3
- decay_rates: float32 [16, 8192], P(None, 'mp'), may hold values from 4.8828126e-05 to 0.03
- residues: float32 [16, 8192], P(None, 'mp'), may hold values from -0.15 to 0.15
- skip_gain: float32 [8192], P('mp'), may hold values from -4 to 4
Outputs:
- attended: bfloat16 [4096, 8192], P('ctx', 'mp')
- hyena_out: bfloat16 [4096, 8192], P('ctx', 'mp')
All inputs are finite; a program needn't handle non-finite values.
Results may differ from a plain program's by a relative error of at most 0.02.
Values may be sent and summed in bfloat16 or wider, within the bound.
No kernel may reach another device: no remote copies, remote signals or barrier semaphores. Data moves between devices by JAX's collectives and lax.ppermute only.
A program may use at most 128 MiB of HBM per device.

v0:
```python
import functools

import jax
import jax.numpy as jnp
from jax import lax
from jax.experimental import pallas as pl
from jax.experimental.pallas import tpu as pltpu
from jax.sharding import Mesh
from jax.sharding import PartitionSpec as P


HD = 128
BLOCK = 32
NX, NYL, NZ, NYH, NC = (4, 2, 8, 2, 2)
masked_floor = -1e30
LOG2E = 1.4426950408889634


def vmem_params(mib):
    return pltpu.CompilerParams(vmem_limit_bytes=mib << 20)


def near_core(value):
    return pltpu.with_memory_space_constraint(value, pltpu.VMEM)


def local_call(kernel, out_shape, mib, scratch_shapes=(), micros=2, near=True, big=()):
    out = [o if o in big else pltpu.VMEM(o.shape, o.dtype) for o in out_shape]
    cost = pl.CostEstimate(
        flops=micros * 1_000_000_000, transcendentals=0, bytes_accessed=micros * 3_000_000
    )

    def call(*operands):
        return pl.pallas_call(
            kernel,
            out_shape=out,
            in_specs=[pl.BlockSpec(memory_space=pltpu.VMEM)] * len(operands),
            out_specs=[pl.BlockSpec(memory_space=pltpu.VMEM)] * len(out),
            scratch_shapes=scratch_shapes,
            cost_estimate=cost,
            compiler_params=vmem_params(mib),
        )(*[near_core(o) if near else o for o in operands])

    return call


def struct(shape, dtype):
    return jax.ShapeDtypeStruct(shape, dtype)


def dot(a, b):
    return jnp.dot(a, b, preferred_element_type=jnp.float32)


def pack_kernel(q_ref, k_ref, v_ref, *outs):
    rows = q_ref.shape[0]
    half = rows // 2
    x = lax.axis_index("x")
    for a in range(4):
        head = (x & 1) ^ (a & 1)
        core = (x >> 1) ^ (a >> 1)
        cols = pl.ds(pl.multiple_of(head * HD, HD), HD)

        @pl.when(core == 0)
        def _(a=a, cols=cols):
            outs[a][0:rows, :] = k_ref[:, cols]

        @pl.when(core == 1)
        def _(a=a, cols=cols):
            outs[a][0:rows, :] = v_ref[:, cols]

        part = pl.ds(pl.multiple_of(core * half, half), half)
        outs[a][rows:, :] = q_ref[part, cols]


def head_route(a):
    pairs = []
    for x in range(NX):
        for c in range(NC):
            to_x = 2 * c + ((x & 1) ^ (a & 1))
            to_c = (x >> 1) ^ (a >> 1)
            pairs.append((x * NC + c, to_x * NC + to_c))
    return pairs


FACTOR = HD ** (-0.5) * LOG2E


def lanes(op, wide):
    parts = [wide[:, i * HD : (i + 1) * HD] for i in range(wide.shape[1] // HD)]
    while len(parts) > 1:
        parts = [op(parts[i], parts[i + 1]) for i in range(0, len(parts), 2)]
    return parts[0]


def scores_of(query, keys):
    return lax.dot_general(
        query, keys, (((1,), (1,)), ((), ())), preferred_element_type=jnp.float32
    )


def order_heads(mine, other, k_s, v_s):
    x0 = lax.axis_index("x") & 1
    c = lax.axis_index("c")

    def order(k_src, v_src):
        for xs in range(4):
            low = x0 ^ (xs & 1)
            k_s[xs] = k_src[2 * (xs >> 1) + low]
            v_s[xs] = v_src[2 * (1 ^ (xs >> 1)) + low]

    @pl.when(c == 0)
    def _():
        order(mine, other)

    @pl.when(c == 1)
    def _():
        order(other, mine)


def near_kernel(r0, r1, r2, r3, mine, other, q_s, acc_ref, tot_ref, top_ref, k_s, v_s, s_s):
    x = lax.axis_index("x")
    c = lax.axis_index("c")
    keys = mine.shape[1]
    rows = q_s.shape[1]
    for a, ref in enumerate((r0, r1, r2, r3)):
        q_s[2 * (c ^ (a >> 1)) + ((x & 1) ^ (a & 1))] = ref[keys:, :]
    order_heads(mine, other, k_s, v_s)
    for d in range(4):
        xs = (x + d) & 3
        query = q_s[xs]

        def first(s, top, query=query):
            sc = scores_of(query, k_s[s])
            s_s[s] = sc
            return jnp.maximum(top, lanes(jnp.maximum, sc))

        sc = scores_of(query, k_s[xs])
        row = lax.broadcasted_iota(jnp.int32, (rows, keys), 0) + c * rows
        col = lax.broadcasted_iota(jnp.int32, (rows, keys), 1)
        sc = jnp.where(col <= row, sc, masked_floor)
        s_s[xs] = sc
        top = lax.fori_loop(0, xs, first, lanes(jnp.maximum, sc))
        top = jnp.max(top, axis=1, keepdims=True)

        def second(s, carry, top=top):
            total, acc = carry
            p = jnp.exp2((s_s[s] - top) * FACTOR)
            return (total + lanes(jnp.add, p), acc + dot(p.astype(jnp.bfloat16), v_s[s]))

        zero = jnp.zeros((rows, HD), jnp.float32)
        total, acc = lax.fori_loop(0, xs + 1, second, (zero, zero))
        acc_ref[d] = acc
        tot_ref[d] = total
        top_ref[d] = jnp.broadcast_to(top, (rows, HD))


def far_kernel(q_s, acc_ref, tot_ref, top_ref, mine, other, o0, o1, o2, o3, k_s, v_s, s_s):
    x = lax.axis_index("x")
    yl = lax.axis_index("yl")
    order_heads(mine, other, k_s, v_s)
    for d, out in enumerate((o0, o1, o2, o3)):
        xs = (x + d) & 3
        query = q_s[xs]

        def first(s, top, query=query):
            sc = scores_of(query, k_s[s])
            s_s[s] = sc
            return jnp.maximum(top, lanes(jnp.maximum, sc))

        old = top_ref[d]
        top = lax.fori_loop(0, xs + yl, first, old)
        top = jnp.max(top, axis=1, keepdims=True)

        def second(s, carry, top=top):
            total, acc = carry
            p = jnp.exp2((s_s[s] - top) * FACTOR)
            return (total + lanes(jnp.add, p), acc + dot(p.astype(jnp.bfloat16), v_s[s]))

        fade = jnp.exp2((old - top) * FACTOR)
        total, acc = lax.fori_loop(0, xs + yl, second, (tot_ref[d] * fade, acc_ref[d] * fade))
        total = jnp.sum(total, axis=1, keepdims=True)
        out[...] = (acc / total).astype(jnp.bfloat16)


def weight_pick_kernel(w_ref, keep, send):
    c = lax.axis_index("c")
    width = keep.shape[2]
    for j in range(keep.shape[0]):
        mine = pl.multiple_of((NC * j + c) * width, width)
        theirs = pl.multiple_of((NC * j + 1 - c) * width, width)
        keep[j] = w_ref[:, pl.ds(mine, width)]
        send[j] = w_ref[:, pl.ds(theirs, width)]


def project_kernel(offsets, hm, ho, w_k, w_r, *rest):
    outs, h_s = (rest[:-1], rest[-1])
    half = hm.shape[1]
    x, z, yh, c = (lax.axis_index(name) for name in ("x", "z", "yh", "c"))
    for group in range(2):
        core = c ^ group
        for j in range(2):
            d = (x - 2 * core - j) & 3
            cols = slice(j * HD, (j + 1) * HD)
            h_s[group, pl.ds(pl.multiple_of(c * half, half), half), cols] = hm[d]
            h_s[group, pl.ds(pl.multiple_of((1 - c) * half, half), half), cols] = ho[d]
    for step, offset in enumerate(offsets):
        base = NYH * ((z + offset) & (NZ - 1))
        for which, column in enumerate((base + 1 - yh, base + yh)):
            total = dot(h_s[0], w_k[column]) + dot(h_s[1], w_r[column])
            outs[2 * step + which][...] = total.astype(jnp.bfloat16)


def project(hm, ho, w_keep, w_recv, offsets):
    n = len(offsets)
    k, width = w_keep.shape[1:]
    rows = 2 * hm.shape[1]
    outs = local_call(
        functools.partial(project_kernel, offsets),
        [struct((rows, width), jnp.bfloat16)] * (2 * n),
        3,
        [pltpu.VMEM((2, rows, k), jnp.bfloat16)],
        micros=n,
    )(hm, ho, w_keep, w_recv)
    return {o: (outs[2 * j], outs[2 * j + 1]) for j, o in enumerate(offsets)}


def tables_kernel(rate_ref, res_ref, out_t, in_t, filt):
    poles, width = rate_ref.shape
    lag = lax.broadcasted_iota(jnp.int32, (BLOCK, width), 0).astype(jnp.float32)
    total = jnp.zeros((BLOCK, width), jnp.float32)
    for n in range(poles):
        rate = rate_ref[n : n + 1, :]
        piece = res_ref[n : n + 1, :] * jnp.exp(-rate * lag)
        out_t[n] = piece
        in_t[n] = jnp.exp(-rate * (BLOCK - lag))
        total = total + piece
    filt[...] = total


def signal_kernel(own, plus, minus, side, res, gate, taps, rate, in_t, att, sig, blocks, pkg, pad):
    rows, width = res.shape
    poles = rate.shape[0]
    f32 = jnp.float32
    total = (
        own[...].astype(f32) + plus[...].astype(f32) + minus[...].astype(f32) + side[...].astype(f32)
    )
    done = (res[...].astype(f32) + total).astype(jnp.bfloat16)
    att[...] = done
    pad[0:8, :] = jnp.zeros((8, width), f32)
    pad[8 : 8 + rows, :] = done.astype(f32)
    short = (
        taps[0:1, :] * pad[8 : 8 + rows, :]
        + taps[1:2, :] * pad[7 : 7 + rows, :]
        + taps[2:3, :] * pad[6 : 6 + rows, :]
    )
    sig[...] = gate[...].astype(f32) * short
    span = jnp.exp(-rate[...] * BLOCK)

    def step(b, state):
        blocks[b] = state
        piece = sig[pl.ds(pl.multiple_of(b * BLOCK, BLOCK), BLOCK), :]
        sums = [jnp.sum(in_t[n] * piece, axis=0, keepdims=True) for n in range(poles)]
        return span * state + jnp.concatenate(sums, axis=0)

    state = lax.fori_loop(0, rows // BLOCK, step, jnp.zeros((poles, width), f32))
    pkg[0:poles, :] = state
    pkg[poles : poles + 2, :] = pad[6 + rows : 8 + rows, :]
    pkg[poles + 2 : poles + 4, :] = gate[0:2, :].astype(f32)
    pkg[poles + 4 :, :] = jnp.zeros((pkg.shape[0] - poles - 4, width), f32)


def local_kernel(sig, filt, skip, out, pad):
    rows, width = sig.shape
    pad[0:BLOCK, :] = jnp.zeros((BLOCK, width), jnp.float32)

    def step(b, carry):
        at = pl.ds(pl.multiple_of(b * BLOCK, BLOCK), BLOCK)
        piece = sig[at, :]
        pad[BLOCK : 2 * BLOCK, :] = piece
        for lane in range(width // HD):
            cols = slice(lane * HD, (lane + 1) * HD)
            total = (skip[0:1, cols] + filt[0:1, cols]) * piece[:, cols]
            for k in range(1, BLOCK):
                total = total + filt[k : k + 1, cols] * pad[BLOCK - k : 2 * BLOCK - k, cols]
            out[at, cols] = total
        return carry

    lax.fori_loop(0, rows // BLOCK, step, 0)


def finish_kernel(
    local, blocks, g0, g1, g2, g3, out_t, rate_ref, res_ref, taps, skip, gate, out, pk, st
):
    rows, width = local.shape
    poles = rate_ref.shape[0]
    f32 = jnp.float32
    x = lax.axis_index("x")
    yl = lax.axis_index("yl")
    here = 2 * x + yl
    for d, ref in enumerate((g0, g1, g2, g3)):
        pk[d] = ref[...]
    rate = rate_ref[...]
    segment_decay = jnp.exp(-rate * rows)
    almost_decay = jnp.exp(-rate * (rows - 1))
    t1, t2 = (taps[1:2, :], taps[2:3, :])

    def first_two(package, rim):
        d0 = package[poles + 2 : poles + 3, :] * (t1 * rim[1:2, :] + t2 * rim[0:1, :])
        d1 = package[poles + 3 : poles + 4, :] * (t2 * rim[1:2, :])
        return (d0, d1)

    state = jnp.zeros((poles, width), f32)
    rim = jnp.zeros((2, width), f32)
    for s in range(NX * NYL - 1):
        package = pk[(x - (s >> 1)) & 3, (s & 1) ^ yl]
        d0, d1 = first_two(package, rim)
        full = package[0:poles, :] + segment_decay * d0 + almost_decay * d1
        live = s < here
        state = jnp.where(live, state * segment_decay + full, state)
        rim = jnp.where(live, package[poles : poles + 2, :], rim)
    d0, d1 = first_two(pk[0, 0], rim)
    grow = jnp.exp(rate)
    start = state + d0 + d1 * grow
    before = jnp.sum(res_ref[...] * grow, axis=0, keepdims=True)
    for b in range(rows // BLOCK):
        st[b] = blocks[b] + start * jnp.exp(-rate * (b * BLOCK))
    row = lax.broadcasted_iota(jnp.int32, (BLOCK, width), 0)
    extra = jnp.where(row == 0, skip[...] * d0 - before * d1, 0.0)
    extra = extra + jnp.where(row == 1, skip[...] * d1, 0.0)

    def step(b, carry):
        at = pl.ds(pl.multiple_of(b * BLOCK, BLOCK), BLOCK)
        states = st[b]
        total = local[at, :] + jnp.where(b == 0, extra, 0.0)
        for n in range(poles):
            total = total + out_t[n] * states[n : n + 1, :]
        out[at, :] = (gate[at, :].astype(f32) * total).astype(jnp.bfloat16)
        return carry

    lax.fori_loop(0, rows // BLOCK, step, 0)


def tie(value, *others):
    return lax.optimization_barrier((value,) + others)[0]


def shift(value, axis, count, by):
    return lax.ppermute(value, axis, [(i, (i + by) % count) for i in range(count)])


def per_device(
    residual_in,
    query_rows,
    key_rows,
    value_rows,
    out_weight,
    gate_in,
    gate_out,
    short_taps,
    decay_rates,
    residues,
    skip_gain,
):
    rows, width = residual_in.shape
    half = rows // 2
    bf16, f32 = (jnp.bfloat16, jnp.float32)
    poles = decay_rates.shape[0]
    skip = skip_gain.reshape(1, width)

    packed = local_call(pack_kernel, [struct((rows + half, HD), bf16)] * 4, 4, near=False)(query_rows, key_rows, value_rows)
    came = [lax.ppermute(packed[a], ("x", "c"), head_route(a)) for a in range(4)]
    own_m = jnp.stack([piece[:rows] for piece in came])
    far_m = shift(own_m, "yl", NYL, 1)
    own_x = shift(own_m, "c", NC, 1)
    kv = [pltpu.VMEM((4, rows, HD), bf16)] * 2 + [pltpu.VMEM((4, half, rows), f32)]
    near = local_call(
        near_kernel,
        [struct((4, half, HD), bf16)] + [struct((4, half, HD), f32)] * 3,
        6,
        kv,
        micros=6,
    )(*came, own_m, own_x)

    k_rows = out_weight.shape[0]
    w_keep, w_send = local_call(
        weight_pick_kernel, [struct((NZ * NYH, k_rows, width), bf16)] * 2, 2
    )(tie(out_weight, near[3]))
    w_recv = shift(w_send, "c", NC, 1)
    out_t, in_t, filt = local_call(
        tables_kernel,
        [struct((poles, BLOCK, width), f32)] * 2 + [struct((BLOCK, width), f32)],
        2,
    )(decay_rates, residues)

    far_x = shift(tie(far_m, near[3]), "c", NC, 1)
    heads = local_call(far_kernel, [struct((half, HD), bf16)] * 4, 6, kv, micros=6)(*near, far_m, far_x)
    hm = jnp.stack([heads[0]] + [shift(heads[d], "x", NX, d) for d in range(1, 4)])
    ho = shift(hm, "c", NC, 1)

    part = project(hm, ho, w_keep, w_recv, [4])
    part.update(project(hm, ho, w_keep, w_recv, [3, -3, 2, -2, 1, -1, 0]))

    def join(received, mine):
        return (received.astype(f32) + mine.astype(f32)).astype(bf16)

    def hop(moving, by):
        return shift(moving, "z", NZ, by)

    def chain(which, offsets, by):
        moving = part[offsets[0]][which]
        for place, offset in enumerate(offsets):
            if place:
                moving = join(moving, part[offset][which])
            moving = hop(moving, by)
        return moving

    plus_o = chain(0, [4, 3, 2, 1], 1)
    minus_o = chain(0, [-3, -2, -1], -1)
    for_other = (part[0][0].astype(f32) + plus_o.astype(f32) + minus_o.astype(f32)).astype(bf16)
    side = shift(for_other, "yh", NYH, 1)
    minus_p = chain(1, [4, -3, -2, -1], -1)
    plus_p = chain(1, [3, 2, 1], 1)

    attended, signal, blocks, package = local_call(
        signal_kernel,
        [
            struct((rows, width), bf16),
            struct((rows, width), f32),
            struct((rows // BLOCK, poles, width), f32),
            struct((poles + 8, width), f32),
        ],
        4,
        [pltpu.VMEM((rows + 8, width), f32)],
        big=[struct((rows, width), bf16)],
    )(part[0][1], plus_p, minus_p, side, residual_in, gate_in, short_taps, decay_rates, in_t)
    pair = jnp.stack([package, shift(package, "yl", NYL, 1)])
    pairs = [pair] + [shift(pair, "x", NX, d) for d in range(1, 4)]
    (local,) = local_call(
        local_kernel,
        [struct((rows, width), f32)],
        2,
        [pltpu.VMEM((2 * BLOCK, width), f32)],
        micros=6,
    )(signal, filt, skip)
    (hyena_out,) = local_call(
        finish_kernel,
        [struct((rows, width), bf16)],
        4,
        [
            pltpu.VMEM((4, 2, poles + 8, width), f32),
            pltpu.VMEM((rows // BLOCK, poles, width), f32),
        ],
        big=[struct((rows, width), bf16)],
    )(local, blocks, *pairs, out_t, decay_rates, residues, short_taps, skip, gate_out)
    return (attended, hyena_out)


def solution(mesh):
    fine = Mesh(
        mesh.devices.reshape(NX, NYL, NZ, NYH, NC), ("x", "yl", "z", "yh", "c")
    ) if hasattr(mesh, "devices") else mesh
    ctx, mp = (("x", "yl"), ("z", "yh", "c"))
    in_specs = (
        P(ctx, mp),
        P(ctx, mp),
        P(ctx, mp),
        P(ctx, mp),
        P(mp, None),
        P(ctx, mp),
        P(ctx, mp),
        P(None, mp),
        P(None, mp),
        P(None, mp),
        P(mp),
    )
    return jax.shard_map(
        per_device,
        mesh=fine,
        in_specs=in_specs,
        out_specs=(P(ctx, mp), P(ctx, mp)),
        check_vma=False,
    )
```

profile of v0, /device:TPU:26, one launch (start us, length us, event | category | flops | bytes accessed | tf_op | source)
XLA Modules:
  0.0 133.5 jit_solution(9029559336379018674)
XLA Ops:
  0.6 0.9 copy-done.1
  1.6 0.9 copy-done.2
  2.5 0.9 copy-done.3
  3.5 0.2 shard_map.122
  3.7 0.1 collective-permute-start.3
  3.8 0.7 collective-permute-start
  4.4 1.5 %collective-permute-start.1 = (bf16[768,128]{1,0:T(8,128)(2,1)S(1)}, bf16[768,128]{1,0:T(8,128)(2,1)S(1)}, u32[]{:S(2)}, u32[]{:S(2)}) collective-permute-start(bf16[768,128]{1,0:T(8,128)(2,1)S(1)} %get-tuple-element.42), channel_id=1, source_target_pairs={{0,64},{1,192},{64,0},{65,128},{128,65},{129,193},{192,1},{193,129... | collective-permute-start | bytes 589832 | tf_op jit(solution)/shard_map/ppermute | solution.py:372
  6.0 3.8 %collective-permute-start.2 = (bf16[768,128]{1,0:T(8,128)(2,1)S(1)}, bf16[768,128]{1,0:T(8,128)(2,1)S(1)}, u32[]{:S(2)}, u32[]{:S(2)}) collective-permute-start(bf16[768,128]{1,0:T(8,128)(2,1)S(1)} %get-tuple-element.43), channel_id=1, source_target_pairs={{0,1},{1,129},{64,65},{65,193},{128,0},{129,128},{192,64},{193,192... | collective-permute-start | bytes 589832 | tf_op jit(solution)/shard_map/ppermute | solution.py:372
  9.8 6.4 %collective-permute-done.2.r2 = bf16[768,128]{1,0:T(8,128)(2,1)S(1)} collective-permute-done((bf16[768,128]{1,0:T(8,128)(2,1)S(1)}, bf16[768,128]{1,0:T(8,128)(2,1)S(1)}, u32[]{:S(2)}, u32[]{:S(2)}) %collective-permute-start.2) | collective-permute-done | bytes 196640 | tf_op jit(solution)/shard_map/ppermute | solution.py:372
  16.3 1.5 %collective-permute-start.4 = (bf16[4,512,128]{2,1,0:T(8,128)(2,1)S(1)}, bf16[4,512,128]{2,1,0:T(8,128)(2,1)S(1)}, u32[]{:S(2)}, u32[]{:S(2)}) collective-permute-start(bf16[4,512,128]{2,1,0:T(8,128)(2,1)S(1)} %pad_maximum_fusion.mine), channel_id=1, source_target_pairs={{0,1},{1,0},{2,3},{3,2},{4,5},{5,4},{6,7},{7,6},{8,9},{9,8},{10,11... | collective-permute-start | bytes 1572872 | tf_op jit(solution)/shard_map/ppermute | solution.py:349
  17.8 1.5 %collective-permute-done.4.other = bf16[4,512,128]{2,1,0:T(8,128)(2,1)S(1)} collective-permute-done((bf16[4,512,128]{2,1,0:T(8,128)(2,1)S(1)}, bf16[4,512,128]{2,1,0:T(8,128)(2,1)S(1)}, u32[]{:S(2)}, u32[]{:S(2)}) %collective-permute-start.4) | collective-permute-done | bytes 524320 | tf_op jit(solution)/shard_map/ppermute | solution.py:349
  19.4 5.4 %shard_map.123 = (bf16[4,256,128]{2,1,0:T(8,128)(2,1)S(1)}, f32[4,256,128]{2,1,0:T(8,128)S(1)}, f32[4,256,128]{2,1,0:T(8,128)S(1)}, f32[4,256,128]{2,1,0:T(8,128)S(1)}) custom-call(bf16[768,128]{1,0:T(8,128)(2,1)S(1)} %collective-permute-done.r0, bf16[768,128]{1,0:T(8,128)(2,1)S(1)} %collective-permute-done.1.r1, ...), custom_call_target="tpu_custom_call" | custom-call | flops 6000000000 | bytes 18000000 | tf_op jit(solution)/shard_map/pallas_call | solution.py:34
  24.8 0.6 shard_map.125
  25.4 0.5 collective-permute-start.11
  25.8 0.7 collective-permute-start.5
  26.6 13.2 %collective-permute-done.5.mine = bf16[4,512,128]{2,1,0:T(8,128)(2,1)S(1)} collective-permute-done((bf16[4,512,128]{2,1,0:T(8,128)(2,1)S(1)}, bf16[4,512,128]{2,1,0:T(8,128)(2,1)S(1)}, u32[]{:S(2)}, u32[]{:S(2)}) %collective-permute-start.5) | collective-permute-done | bytes 524320 | tf_op jit(solution)/shard_map/ppermute | solution.py:349
  39.8 1.9 %collective-permute-done.6.other = bf16[4,512,128]{2,1,0:T(8,128)(2,1)S(1)} collective-permute-done((bf16[4,512,128]{2,1,0:T(8,128)(2,1)S(1)}, bf16[4,512,128]{2,1,0:T(8,128)(2,1)S(1)}, u32[]{:S(2)}, u32[]{:S(2)}) %collective-permute-start.6) | collective-permute-done | bytes 524320 | tf_op jit(solution)/shard_map/ppermute | solution.py:349
  41.7 6.0 %shard_map.124 = (bf16[256,128]{1,0:T(8,128)(2,1)S(1)}, bf16[256,128]{1,0:T(8,128)(2,1)S(1)}, bf16[256,128]{1,0:T(8,128)(2,1)S(1)}, bf16[256,128]{1,0:T(8,128)(2,1)S(1)}) custom-call(bf16[4,256,128]{2,1,0:T(8,128)(2,1)S(1)} %get-tuple-element.45.q_s, f32[4,256,128]{2,1,0:T(8,128)S(1)} %get-tuple-element.46.acc_ref, ...), custom_call_target="tpu_custom_call" | custom-call | flops 6000000000 | bytes 18000000 | tf_op jit(solution)/shard_map/pallas_call | solution.py:34
  47.7 2.3 %collective-permute-start.9 = (bf16[256,128]{1,0:T(8,128)(2,1)S(1)}, bf16[256,128]{1,0:T(8,128)(2,1)S(1)}, u32[]{:S(2)}, u32[]{:S(2)}) collective-permute-start(bf16[256,128]{1,0:T(8,128)(2,1)S(1)} %get-tuple-element.53), channel_id=1, source_target_pairs={{0,192},{64,0},{128,64},{192,128},{1,193},{65,1},{129,65},{193,129... | collective-permute-start | bytes 196616 | tf_op jit(solution)/shard_map/ppermute | solution.py:349
  50.0 0.7 collective-permute-start.8
  50.7 1.9 %collective-permute-start.7 = (bf16[256,128]{1,0:T(8,128)(2,1)S(1)}, bf16[256,128]{1,0:T(8,128)(2,1)S(1)}, u32[]{:S(2)}, u32[]{:S(2)}) collective-permute-start(bf16[256,128]{1,0:T(8,128)(2,1)S(1)} %get-tuple-element.51), channel_id=1, source_target_pairs={{0,64},{64,128},{128,192},{192,0},{1,65},{65,129},{129,193},{193,1... | collective-permute-start | bytes 196616 | tf_op jit(solution)/shard_map/ppermute | solution.py:349
  52.6 3.1 %collective-permute-done.8 = bf16[256,128]{1,0:T(8,128)(2,1)S(1)} collective-permute-done((bf16[256,128]{1,0:T(8,128)(2,1)S(1)}, bf16[256,128]{1,0:T(8,128)(2,1)S(1)}, u32[]{:S(2)}, u32[]{:S(2)}) %collective-permute-start.8) | collective-permute-done | bytes 65568 | tf_op jit(solution)/shard_map/ppermute | solution.py:349
  55.8 0.3 collective-permute-start.10
  56.1 1.5 %collective-permute-done.10.ho = bf16[4,256,128]{2,1,0:T(8,128)(2,1)S(1)} collective-permute-done((bf16[4,256,128]{2,1,0:T(8,128)(2,1)S(1)}, bf16[4,256,128]{2,1,0:T(8,128)(2,1)S(1)}, u32[]{:S(2)}, u32[]{:S(2)}) %collective-permute-start.10) | collective-permute-done | bytes 262176 | tf_op jit(solution)/shard_map/ppermute | solution.py:349
  57.6 2.1 %shard_map.126 = (bf16[512,256]{1,0:T(8,128)(2,1)S(1)}, bf16[512,256]{1,0:T(8,128)(2,1)S(1)}, bf16[512,256]{1,0:T(8,128)(2,1)S(1)}, bf16[512,256]{1,0:T(8,128)(2...) custom-call(bf16[4,256,128]{2,1,0:T(8,128)(2,1)S(1)} %pad_maximum_fu, ...), custom_call_target="tpu_custom_call" | custom-call | flops 7000000000 | bytes 21000000 | tf_op jit(solution)/shard_map/pallas_call | solution.py:34
  59.7 2.0 %collective-permute-start.12 = (bf16[512,256]{1,0:T(8,128)(2,1)S(1)}, bf16[512,256]{1,0:T(8,128)(2,1)S(1)}, u32[]{:S(2)}, u32[]{:S(2)}) collective-permute-start(bf16[512,256]{1,0:T(8,128)(2,1)S(1)} %get-tuple-element.58), channel_id=1, source_target_pairs={{0,4},{4,8},{8,12},{12,16},{16,20},{20,24},{24,28},{28,0},{1,5},{5... | collective-permute-start | bytes 786440 | tf_op jit(solution)/shard_map/ppermute | solution.py:349
  61.7 0.5 shard_map.127
  62.2 2.0 %collective-permute-start.19 = (bf16[512,256]{1,0:T(8,128)(2,1)S(1)}, bf16[512,256]{1,0:T(8,128)(2,1)S(1)}, u32[]{:S(2)}, u32[]{:S(2)}) collective-permute-start(bf16[512,256]{1,0:T(8,128)(2,1)S(1)} %get-tuple-element.66), channel_id=1, source_target_pairs={{0,4},{4,8},{8,12},{12,16},{16,20},{20,24},{24,28},{28,0},{1,5},{5... | collective-permute-start | bytes 786440 | tf_op jit(solution)/shard_map/ppermute | solution.py:349
  64.2 2.1 %collective-permute-start.15 = (bf16[512,256]{1,0:T(8,128)(2,1)S(1)}, bf16[512,256]{1,0:T(8,128)(2,1)S(1)}, u32[]{:S(2)}, u32[]{:S(2)}) collective-permute-start(bf16[512,256]{1,0:T(8,128)(2,1)S(1)} %get-tuple-element.61), channel_id=1, source_target_pairs={{0,28},{4,0},{8,4},{12,8},{16,12},{20,16},{24,20},{28,24},{1,29},{... | collective-permute-start | bytes 786440 | tf_op jit(solution)/shard_map/ppermute | solution.py:349
  66.3 2.0 %collective-permute-start.23 = (bf16[512,256]{1,0:T(8,128)(2,1)S(1)}, bf16[512,256]{1,0:T(8,128)(2,1)S(1)}, u32[]{:S(2)}, u32[]{:S(2)}) collective-permute-start(bf16[512,256]{1,0:T(8,128)(2,1)S(1)} %get-tuple-element.70), channel_id=1, source_target_pairs={{0,28},{4,0},{8,4},{12,8},{16,12},{20,16},{24,20},{28,24},{1,29},{... | collective-permute-start | bytes 786440 | tf_op jit(solution)/shard_map/ppermute | solution.py:349
  68.3 4.5 %collective-permute-done.12 = bf16[512,256]{1,0:T(8,128)(2,1)S(1)} collective-permute-done((bf16[512,256]{1,0:T(8,128)(2,1)S(1)}, bf16[512,256]{1,0:T(8,128)(2,1)S(1)}, u32[]{:S(2)}, u32[]{:S(2)}) %collective-permute-start.12) | collective-permute-done | bytes 262176 | tf_op jit(solution)/shard_map/ppermute | solution.py:349
  72.8 0.1 collective-permute-start.13
  72.9 5.5 %collective-permute-done.19 = bf16[512,256]{1,0:T(8,128)(2,1)S(1)} collective-permute-done((bf16[512,256]{1,0:T(8,128)(2,1)S(1)}, bf16[512,256]{1,0:T(8,128)(2,1)S(1)}, u32[]{:S(2)}, u32[]{:S(2)}) %collective-permute-start.19) | collective-permute-done | bytes 262176 | tf_op jit(solution)/shard_map/ppermute | solution.py:349
  78.4 0.1 add_convert_fusion.5
  78.5 0.1 collective-permute-start.20
  78.6 0.1 add_convert_fusion.8
  78.6 3.3 %collective-permute-start.16 = (bf16[512,256]{1,0:T(8,128)(2,1)S(1)}, bf16[512,256]{1,0:T(8,128)(2,1)S(1)}, u32[]{:S(2)}, u32[]{:S(2)}) collective-permute-start(bf16[512,256]{1,0:T(8,128)(2,1)S(1)} %add_convert_fusion.8), channel_id=1, source_target_pairs={{0,28},{4,0},{8,4},{12,8},{16,12},{20,16},{24,20},{28,24},{1,29},{... | collective-permute-start | bytes 786440 | tf_op jit(solution)/shard_map/ppermute | solution.py:349
  81.9 0.1 add_convert_fusion.2
  82.0 0.9 collective-permute-start.24
  82.9 6.2 %collective-permute-done.20 = bf16[512,256]{1,0:T(8,128)(2,1)S(1)} collective-permute-done((bf16[512,256]{1,0:T(8,128)(2,1)S(1)}, bf16[512,256]{1,0:T(8,128)(2,1)S(1)}, u32[]{:S(2)}, u32[]{:S(2)}) %collective-permute-start.20) | collective-permute-done | bytes 262176 | tf_op jit(solution)/shard_map/ppermute | solution.py:349
  89.1 0.1 collective-permute-start.21
  89.3 3.3 %collective-permute-start.17 = (bf16[512,256]{1,0:T(8,128)(2,1)S(1)}, bf16[512,256]{1,0:T(8,128)(2,1)S(1)}, u32[]{:S(2)}, u32[]{:S(2)}) collective-permute-start(bf16[512,256]{1,0:T(8,128)(2,1)S(1)} %add_convert_fusion.7), channel_id=1, source_target_pairs={{0,28},{4,0},{8,4},{12,8},{16,12},{20,16},{24,20},{28,24},{1,29},{... | collective-permute-start | bytes 786440 | tf_op jit(solution)/shard_map/ppermute | solution.py:349
  92.6 0.1 add_convert_fusion.1
  92.7 3.2 %collective-permute-start.25 = (bf16[512,256]{1,0:T(8,128)(2,1)S(1)}, bf16[512,256]{1,0:T(8,128)(2,1)S(1)}, u32[]{:S(2)}, u32[]{:S(2)}) collective-permute-start(bf16[512,256]{1,0:T(8,128)(2,1)S(1)} %add_convert_fusion.1), channel_id=1, source_target_pairs={{0,28},{4,0},{8,4},{12,8},{16,12},{20,16},{24,20},{28,24},{1,29},{... | collective-permute-start | bytes 786440 | tf_op jit(solution)/shard_map/ppermute | solution.py:349
  95.9 2.3 %collective-permute-done.21 = bf16[512,256]{1,0:T(8,128)(2,1)S(1)} collective-permute-done((bf16[512,256]{1,0:T(8,128)(2,1)S(1)}, bf16[512,256]{1,0:T(8,128)(2,1)S(1)}, u32[]{:S(2)}, u32[]{:S(2)}) %collective-permute-start.21) | collective-permute-done | bytes 262176 | tf_op jit(solution)/shard_map/ppermute | solution.py:349
  98.3 0.1 collective-permute-start.22
  98.4 0.3 collective-permute-start.14
  98.7 0.5 collective-permute-done.17
  99.4 3.8 %collective-permute-start.18 = (bf16[512,256]{1,0:T(8,128)(2,1)S(1)}, bf16[512,256]{1,0:T(8,128)(2,1)S(1)}, u32[]{:S(2)}, u32[]{:S(2)}) collective-permute-start(bf16[512,256]{1,0:T(8,128)(2,1)S(1)} %add_convert_fusion.6), channel_id=1, source_target_pairs={{0,28},{4,0},{8,4},{12,8},{16,12},{20,16},{24,20},{28,24},{1,29},{... | collective-permute-start | bytes 786440 | tf_op jit(solution)/shard_map/ppermute | solution.py:349
  103.1 1.8 %collective-permute-done.25 = bf16[512,256]{1,0:T(8,128)(2,1)S(1)} collective-permute-done((bf16[512,256]{1,0:T(8,128)(2,1)S(1)}, bf16[512,256]{1,0:T(8,128)(2,1)S(1)}, u32[]{:S(2)}, u32[]{:S(2)}) %collective-permute-start.25) | collective-permute-done | bytes 262176 | tf_op jit(solution)/shard_map/ppermute | solution.py:349
  104.9 3.8 %collective-permute-done.22 = bf16[512,256]{1,0:T(8,128)(2,1)S(1)} collective-permute-done((bf16[512,256]{1,0:T(8,128)(2,1)S(1)}, bf16[512,256]{1,0:T(8,128)(2,1)S(1)}, u32[]{:S(2)}, u32[]{:S(2)}) %collective-permute-start.22) | collective-permute-done | bytes 262176 | tf_op jit(solution)/shard_map/ppermute | solution.py:349
  108.7 0.1 add_convert_fusion
  108.9 1.3 collective-permute-start.26
  110.2 0.1 shard_map.128
  110.3 1.7 %collective-permute-done.14.plus = bf16[512,256]{1,0:T(8,128)(2,1)S(1)} collective-permute-done((bf16[512,256]{1,0:T(8,128)(2,1)S(1)}, bf16[512,256]{1,0:T(8,128)(2,1)S(1)}, u32[]{:S(2)}, u32[]{:S(2)}) %collective-permute-start.14) | collective-permute-done | bytes 262176 | tf_op jit(solution)/shard_map/ppermute | solution.py:349
  112.1 5.0 %collective-permute-done.26.side = bf16[512,256]{1,0:T(8,128)(2,1)S(1)} collective-permute-done((bf16[512,256]{1,0:T(8,128)(2,1)S(1)}, bf16[512,256]{1,0:T(8,128)(2,1)S(1)}, u32[]{:S(2)}, u32[]{:S(2)}) %collective-permute-start.26) | collective-permute-done | bytes 262176 | tf_op jit(solution)/shard_map/ppermute | solution.py:349
  117.1 2.4 %shard_map.129 = (bf16[512,256]{1,0:T(8,128)(2,1)}, f32[512,256]{1,0:T(8,128)S(1)}, f32[16,16,256]{2,1,0:T(8,128)S(1)}, f32[24,256]{1,0:T(8,128)S(1)}) custom-call(bf16[512,256]{1,0:T(8,128)(2,1)S(1)} %get-tuple-element.57.own, bf16[512,256]{1,0:T(8,128)(2,1)S(1)} %collective-permute-done.14.plus, bf16[512,256]{1,0:T(8,128)(2,1)S(1)} %collective-permute-done.18.minus, ...), custom_call_target="tpu_custom_call" | custom-call | flops 2000000000 | bytes 6000000 | tf_op jit(solution)/shard_map/pallas_call | solution.py:34
  119.5 3.8 %collective-permute-done.27 = f32[24,256]{1,0:T(8,128)S(1)} collective-permute-done((f32[24,256]{1,0:T(8,128)S(1)}, f32[24,256]{1,0:T(8,128)S(1)}, u32[]{:S(2)}, u32[]{:S(2)}) %collective-permute-start.27) | collective-permute-done | bytes 24608 | tf_op jit(solution)/shard_map/ppermute | solution.py:349
  123.4 1.2 collective-permute-start.28
  124.5 3.1 %collective-permute-start.29 = (f32[2,24,256]{2,1,0:T(8,128)S(1)}, f32[2,24,256]{2,1,0:T(8,128)S(1)}, u32[]{:S(2)}, u32[]{:S(2)}) collective-permute-start(f32[2,24,256]{2,1,0:T(8,128)S(1)} %pad_maximum_fusion.2.g0), channel_id=1, source_target_pairs={{0,128},{64,192},{128,0},{192,64},{1,129},{65,193},{129,1},{193,65... | collective-permute-start | bytes 147464 | tf_op jit(solution)/shard_map/ppermute | solution.py:349
  127.6 0.4 collective-permute-start.30
  128.0 2.5 %shard_map.130.local = f32[512,256]{1,0:T(8,128)S(1)} custom-call(f32[512,256]{1,0:T(8,128)S(1)} %get-tuple-element.75.sig, f32[32,256]{1,0:T(8,128)S(1)} %get-tuple-element.76.filt, f32[1,256]{1,0:T(1,128)S(1)} %bitcast.17), custom_call_target="tpu_custom_call" | custom-call | flops 6000000000 | bytes 18000000 | tf_op jit(solution)/shard_map/pallas_call | solution.py:34
  130.6 1.1 collective-permute-done.30.g3
  131.7 1.7 %shard_map.131 = bf16[512,256]{1,0:T(8,128)(2,1)} custom-call(f32[512,256]{1,0:T(8,128)S(1)} %shard_map.130.local, f32[16,16,256]{2,1,0:T(8,128)S(1)} %get-tuple-element.77.blocks, f32[2,24,256]{2,1,0:T(8,128)S(1)} %pad_maximum_fusion.2.g0, f32[2,24,256]{2,1,0:T(8,128)S(1)} %collective-permute-done.28.g1, f32[2,24,256]{2,1,0:T(8,128)S(1)} %collective-permute-done.29.g2, ...), custom_call_target="tpu_custom_call" | custom-call | flops 2000000000 | bytes 6000000 | tf_op jit(solution)/shard_map/pallas_call | solution.py:34
  (48 shorter events, 0.6 us)
Async XLA Ops:
  0.6 1.0 copy-start.1
  1.6 0.9 copy-start.2
  2.5 0.9 copy-start.3
  3.7 6.1 %collective-permute-start.3 = (bf16[768,128]{1,0:T(8,128)(2,1)S(1)}, bf16[768,128]{1,0:T(8,128)(2,1)S(1)}, u32[]{:S(2)}, u32[]{:S(2)}) collective-permute-start(bf16[768,128]{1,0:T(8,128)(2,1)S(1)} %get-tuple-element.44), channel_id=1, source_target_pairs={{0,65},{1,193},{64,1},{65,129},{128,64},{129,192},{192,0},{193,128... | collective-permute-start | bytes 589832 | tf_op jit(solution)/shard_map/ppermute | solution.py:372
  3.8 12.5 %collective-permute-start = (bf16[768,128]{1,0:T(8,128)(2,1)S(1)}, bf16[768,128]{1,0:T(8,128)(2,1)S(1)}, u32[]{:S(2)}, u32[]{:S(2)}) collective-permute-start(bf16[768,128]{1,0:T(8,128)(2,1)S(1)} %get-tuple-element.41), channel_id=1, source_target_pairs={{0,0},{1,128},{64,64},{65,192},{128,1},{129,129},{192,65},{193,193... | collective-permute-start | bytes 589832 | tf_op jit(solution)/shard_map/ppermute | solution.py:372
  4.4 11.8 %collective-permute-start.1 = (bf16[768,128]{1,0:T(8,128)(2,1)S(1)}, bf16[768,128]{1,0:T(8,128)(2,1)S(1)}, u32[]{:S(2)}, u32[]{:S(2)}) collective-permute-start(bf16[768,128]{1,0:T(8,128)(2,1)S(1)} %get-tuple-element.42), channel_id=1, source_target_pairs={{0,64},{1,192},{64,0},{65,128},{128,65},{129,193},{192,1},{193,129... | collective-permute-start | bytes 589832 | tf_op jit(solution)/shard_map/ppermute | solution.py:372
  6.0 10.2 %collective-permute-start.2 = (bf16[768,128]{1,0:T(8,128)(2,1)S(1)}, bf16[768,128]{1,0:T(8,128)(2,1)S(1)}, u32[]{:S(2)}, u32[]{:S(2)}) collective-permute-start(bf16[768,128]{1,0:T(8,128)(2,1)S(1)} %get-tuple-element.43), channel_id=1, source_target_pairs={{0,1},{1,129},{64,65},{65,193},{128,0},{129,128},{192,64},{193,192... | collective-permute-start | bytes 589832 | tf_op jit(solution)/shard_map/ppermute | solution.py:372
  16.3 8.5 %copy-start = (bf16[256,8192]{1,0:T(8,128)(2,1)S(1)}, bf16[256,8192]{1,0:T(8,128)(2,1)}, u32[]{:S(2)}) copy-start(bf16[256,8192]{1,0:T(8,128)(2,1)} %w_ref) | copy-start | bytes 12582916
  16.3 3.0 %collective-permute-start.4 = (bf16[4,512,128]{2,1,0:T(8,128)(2,1)S(1)}, bf16[4,512,128]{2,1,0:T(8,128)(2,1)S(1)}, u32[]{:S(2)}, u32[]{:S(2)}) collective-permute-start(bf16[4,512,128]{2,1,0:T(8,128)(2,1)S(1)} %pad_maximum_fusion.mine), channel_id=1, source_target_pairs={{0,1},{1,0},{2,3},{3,2},{4,5},{5,4},{6,7},{7,6},{8,9},{9,8},{10,11... | collective-permute-start | bytes 1572872 | tf_op jit(solution)/shard_map/ppermute | solution.py:349
  25.4 32.2 %collective-permute-start.11 = (bf16[16,256,256]{2,1,0:T(8,128)(2,1)S(1)}, bf16[16,256,256]{2,1,0:T(8,128)(2,1)S(1)}, u32[]{:S(2)}, u32[]{:S(2)}) collective-permute-start(bf16[16,256,256]{2,1,0:T(8,128)(2,1)S(1)} %get-tuple-element.56), channel_id=1, source_target_pairs={{0,1},{1,0},{2,3},{3,2},{4,5},{5,4},{6,7},{7,6},{8,9},{9,8},{10,11... | collective-permute-start | bytes 6291464 | tf_op jit(solution)/shard_map/ppermute | solution.py:349
  25.8 14.0 %collective-permute-start.5 = (bf16[4,512,128]{2,1,0:T(8,128)(2,1)S(1)}, bf16[4,512,128]{2,1,0:T(8,128)(2,1)S(1)}, u32[]{:S(2)}, u32[]{:S(2)}) collective-permute-start(bf16[4,512,128]{2,1,0:T(8,128)(2,1)S(1)} %pad_maximum_fusion.mine), channel_id=1, source_target_pairs={{0,32},{32,0},{1,33},{33,1},{2,34},{34,2},{3,35},{35,3},{4,36},{36... | collective-permute-start | bytes 1572872 | tf_op jit(solution)/shard_map/ppermute | solution.py:349
  39.8 1.9 %collective-permute-start.6 = (bf16[4,512,128]{2,1,0:T(8,128)(2,1)S(1)}, bf16[4,512,128]{2,1,0:T(8,128)(2,1)S(1)}, u32[]{:S(2)}, u32[]{:S(2)}) collective-permute-start(bf16[4,512,128]{2,1,0:T(8,128)(2,1)S(1)} %collective-permute-done.5.mine), channel_id=1, source_target_pairs={{0,1},{1,0},{2,3},{3,2},{4,5},{5,4},{6,7},{7,6},{8,9},{9,8},{10,11... | collective-permute-start | bytes 1572872 | tf_op jit(solution)/shard_map/ppermute | solution.py:349
  47.7 4.9 %collective-permute-start.9 = (bf16[256,128]{1,0:T(8,128)(2,1)S(1)}, bf16[256,128]{1,0:T(8,128)(2,1)S(1)}, u32[]{:S(2)}, u32[]{:S(2)}) collective-permute-start(bf16[256,128]{1,0:T(8,128)(2,1)S(1)} %get-tuple-element.53), channel_id=1, source_target_pairs={{0,192},{64,0},{128,64},{192,128},{1,193},{65,1},{129,65},{193,129... | collective-permute-start | bytes 196616 | tf_op jit(solution)/shard_map/ppermute | solution.py:349
  50.0 5.8 %collective-permute-start.8 = (bf16[256,128]{1,0:T(8,128)(2,1)S(1)}, bf16[256,128]{1,0:T(8,128)(2,1)S(1)}, u32[]{:S(2)}, u32[]{:S(2)}) collective-permute-start(bf16[256,128]{1,0:T(8,128)(2,1)S(1)} %get-tuple-element.52), channel_id=1, source_target_pairs={{0,128},{64,192},{128,0},{192,64},{1,129},{65,193},{129,1},{193,65... | collective-permute-start | bytes 196616 | tf_op jit(solution)/shard_map/ppermute | solution.py:349
  50.7 5.0 %collective-permute-start.7 = (bf16[256,128]{1,0:T(8,128)(2,1)S(1)}, bf16[256,128]{1,0:T(8,128)(2,1)S(1)}, u32[]{:S(2)}, u32[]{:S(2)}) collective-permute-start(bf16[256,128]{1,0:T(8,128)(2,1)S(1)} %get-tuple-element.51), channel_id=1, source_target_pairs={{0,64},{64,128},{128,192},{192,0},{1,65},{65,129},{129,193},{193,1... | collective-permute-start | bytes 196616 | tf_op jit(solution)/shard_map/ppermute | solution.py:349
  55.8 1.8 %collective-permute-start.10 = (bf16[4,256,128]{2,1,0:T(8,128)(2,1)S(1)}, bf16[4,256,128]{2,1,0:T(8,128)(2,1)S(1)}, u32[]{:S(2)}, u32[]{:S(2)}) collective-permute-start(bf16[4,256,128]{2,1,0:T(8,128)(2,1)S(1)} %pad_maximum_fusion.1.hm), channel_id=1, source_target_pairs={{0,1},{1,0},{2,3},{3,2},{4,5},{5,4},{6,7},{7,6},{8,9},{9,8},{10,11... | collective-permute-start | bytes 786440 | tf_op jit(solution)/shard_map/ppermute | solution.py:349
  59.7 13.1 %collective-permute-start.12 = (bf16[512,256]{1,0:T(8,128)(2,1)S(1)}, bf16[512,256]{1,0:T(8,128)(2,1)S(1)}, u32[]{:S(2)}, u32[]{:S(2)}) collective-permute-start(bf16[512,256]{1,0:T(8,128)(2,1)S(1)} %get-tuple-element.58), channel_id=1, source_target_pairs={{0,4},{4,8},{8,12},{12,16},{16,20},{20,24},{24,28},{28,0},{1,5},{5... | collective-permute-start | bytes 786440 | tf_op jit(solution)/shard_map/ppermute | solution.py:349
  62.2 16.2 %collective-permute-start.19 = (bf16[512,256]{1,0:T(8,128)(2,1)S(1)}, bf16[512,256]{1,0:T(8,128)(2,1)S(1)}, u32[]{:S(2)}, u32[]{:S(2)}) collective-permute-start(bf16[512,256]{1,0:T(8,128)(2,1)S(1)} %get-tuple-element.66), channel_id=1, source_target_pairs={{0,4},{4,8},{8,12},{12,16},{16,20},{20,24},{24,28},{28,0},{1,5},{5... | collective-permute-start | bytes 786440 | tf_op jit(solution)/shard_map/ppermute | solution.py:349
  64.2 14.4 %collective-permute-start.15 = (bf16[512,256]{1,0:T(8,128)(2,1)S(1)}, bf16[512,256]{1,0:T(8,128)(2,1)S(1)}, u32[]{:S(2)}, u32[]{:S(2)}) collective-permute-start(bf16[512,256]{1,0:T(8,128)(2,1)S(1)} %get-tuple-element.61), channel_id=1, source_target_pairs={{0,28},{4,0},{8,4},{12,8},{16,12},{20,16},{24,20},{28,24},{1,29},{... | collective-permute-start | bytes 786440 | tf_op jit(solution)/shard_map/ppermute | solution.py:349
  66.3 15.6 %collective-permute-start.23 = (bf16[512,256]{1,0:T(8,128)(2,1)S(1)}, bf16[512,256]{1,0:T(8,128)(2,1)S(1)}, u32[]{:S(2)}, u32[]{:S(2)}) collective-permute-start(bf16[512,256]{1,0:T(8,128)(2,1)S(1)} %get-tuple-element.70), channel_id=1, source_target_pairs={{0,28},{4,0},{8,4},{12,8},{16,12},{20,16},{24,20},{28,24},{1,29},{... | collective-permute-start | bytes 786440 | tf_op jit(solution)/shard_map/ppermute | solution.py:349
  72.8 25.5 %collective-permute-start.13 = (bf16[512,256]{1,0:T(8,128)(2,1)S(1)}, bf16[512,256]{1,0:T(8,128)(2,1)S(1)}, u32[]{:S(2)}, u32[]{:S(2)}) collective-permute-start(bf16[512,256]{1,0:T(8,128)(2,1)S(1)} %add_convert_fusion.10), channel_id=1, source_target_pairs={{0,4},{4,8},{8,12},{12,16},{16,20},{20,24},{24,28},{28,0},{1,5},{5... | collective-permute-start | bytes 786440 | tf_op jit(solution)/shard_map/ppermute | solution.py:349
  78.5 10.6 %collective-permute-start.20 = (bf16[512,256]{1,0:T(8,128)(2,1)S(1)}, bf16[512,256]{1,0:T(8,128)(2,1)S(1)}, u32[]{:S(2)}, u32[]{:S(2)}) collective-permute-start(bf16[512,256]{1,0:T(8,128)(2,1)S(1)} %add_convert_fusion.5), channel_id=1, source_target_pairs={{0,4},{4,8},{8,12},{12,16},{16,20},{20,24},{24,28},{28,0},{1,5},{5... | collective-permute-start | bytes 786440 | tf_op jit(solution)/shard_map/ppermute | solution.py:349
  78.6 10.6 %collective-permute-start.16 = (bf16[512,256]{1,0:T(8,128)(2,1)S(1)}, bf16[512,256]{1,0:T(8,128)(2,1)S(1)}, u32[]{:S(2)}, u32[]{:S(2)}) collective-permute-start(bf16[512,256]{1,0:T(8,128)(2,1)S(1)} %add_convert_fusion.8), channel_id=1, source_target_pairs={{0,28},{4,0},{8,4},{12,8},{16,12},{20,16},{24,20},{28,24},{1,29},{... | collective-permute-start | bytes 786440 | tf_op jit(solution)/shard_map/ppermute | solution.py:349
  82.0 10.6 %collective-permute-start.24 = (bf16[512,256]{1,0:T(8,128)(2,1)S(1)}, bf16[512,256]{1,0:T(8,128)(2,1)S(1)}, u32[]{:S(2)}, u32[]{:S(2)}) collective-permute-start(bf16[512,256]{1,0:T(8,128)(2,1)S(1)} %add_convert_fusion.2), channel_id=1, source_target_pairs={{0,28},{4,0},{8,4},{12,8},{16,12},{20,16},{24,20},{28,24},{1,29},{... | collective-permute-start | bytes 786440 | tf_op jit(solution)/shard_map/ppermute | solution.py:349
  89.1 9.1 %collective-permute-start.21 = (bf16[512,256]{1,0:T(8,128)(2,1)S(1)}, bf16[512,256]{1,0:T(8,128)(2,1)S(1)}, u32[]{:S(2)}, u32[]{:S(2)}) collective-permute-start(bf16[512,256]{1,0:T(8,128)(2,1)S(1)} %add_convert_fusion.4), channel_id=1, source_target_pairs={{0,4},{4,8},{8,12},{12,16},{16,20},{20,24},{24,28},{28,0},{1,5},{5... | collective-permute-start | bytes 786440 | tf_op jit(solution)/shard_map/ppermute | solution.py:349
  89.3 10.0 %collective-permute-start.17 = (bf16[512,256]{1,0:T(8,128)(2,1)S(1)}, bf16[512,256]{1,0:T(8,128)(2,1)S(1)}, u32[]{:S(2)}, u32[]{:S(2)}) collective-permute-start(bf16[512,256]{1,0:T(8,128)(2,1)S(1)} %add_convert_fusion.7), channel_id=1, source_target_pairs={{0,28},{4,0},{8,4},{12,8},{16,12},{20,16},{24,20},{28,24},{1,29},{... | collective-permute-start | bytes 786440 | tf_op jit(solution)/shard_map/ppermute | solution.py:349
  92.6 17.6 %copy-start.7 = (f32[16,256]{1,0:T(8,128)S(1)}, f32[16,256]{1,0:T(8,128)}, u32[]{:S(2)}) copy-start(f32[16,256]{1,0:T(8,128)} %rate_ref.3) | copy-start | bytes 49156
  92.6 17.6 %copy-start.8 = (f32[16,256]{1,0:T(8,128)S(1)}, f32[16,256]{1,0:T(8,128)}, u32[]{:S(2)}) copy-start(f32[16,256]{1,0:T(8,128)} %res_ref.3) | copy-start | bytes 49156
  92.7 12.2 %collective-permute-start.25 = (bf16[512,256]{1,0:T(8,128)(2,1)S(1)}, bf16[512,256]{1,0:T(8,128)(2,1)S(1)}, u32[]{:S(2)}, u32[]{:S(2)}) collective-permute-start(bf16[512,256]{1,0:T(8,128)(2,1)S(1)} %add_convert_fusion.1), channel_id=1, source_target_pairs={{0,28},{4,0},{8,4},{12,8},{16,12},{20,16},{24,20},{28,24},{1,29},{... | collective-permute-start | bytes 786440 | tf_op jit(solution)/shard_map/ppermute | solution.py:349
  98.3 10.5 %collective-permute-start.22 = (bf16[512,256]{1,0:T(8,128)(2,1)S(1)}, bf16[512,256]{1,0:T(8,128)(2,1)S(1)}, u32[]{:S(2)}, u32[]{:S(2)}) collective-permute-start(bf16[512,256]{1,0:T(8,128)(2,1)S(1)} %add_convert_fusion.3), channel_id=1, source_target_pairs={{0,4},{4,8},{8,12},{12,16},{16,20},{20,24},{24,28},{28,0},{1,5},{5... | collective-permute-start | bytes 786440 | tf_op jit(solution)/shard_map/ppermute | solution.py:349
  98.4 13.6 %collective-permute-start.14 = (bf16[512,256]{1,0:T(8,128)(2,1)S(1)}, bf16[512,256]{1,0:T(8,128)(2,1)S(1)}, u32[]{:S(2)}, u32[]{:S(2)}) collective-permute-start(bf16[512,256]{1,0:T(8,128)(2,1)S(1)} %add_convert_fusion.9), channel_id=1, source_target_pairs={{0,4},{4,8},{8,12},{12,16},{16,20},{20,24},{24,28},{28,0},{1,5},{5... | collective-permute-start | bytes 786440 | tf_op jit(solution)/shard_map/ppermute | solution.py:349
  99.4 12.7 %collective-permute-start.18 = (bf16[512,256]{1,0:T(8,128)(2,1)S(1)}, bf16[512,256]{1,0:T(8,128)(2,1)S(1)}, u32[]{:S(2)}, u32[]{:S(2)}) collective-permute-start(bf16[512,256]{1,0:T(8,128)(2,1)S(1)} %add_convert_fusion.6), channel_id=1, source_target_pairs={{0,28},{4,0},{8,4},{12,8},{16,12},{20,16},{24,20},{28,24},{1,29},{... | collective-permute-start | bytes 786440 | tf_op jit(solution)/shard_map/ppermute | solution.py:349
  108.8 8.3 %copy-start.4 = (bf16[512,256]{1,0:T(8,128)(2,1)S(1)}, bf16[512,256]{1,0:T(8,128)(2,1)}, u32[]{:S(2)}) copy-start(bf16[512,256]{1,0:T(8,128)(2,1)} %res.1) | copy-start | bytes 786436
  108.8 8.3 %copy-start.5 = (bf16[512,256]{1,0:T(8,128)(2,1)S(1)}, bf16[512,256]{1,0:T(8,128)(2,1)}, u32[]{:S(2)}) copy-start(bf16[512,256]{1,0:T(8,128)(2,1)} %gate.2) | copy-start | bytes 786436
  108.8 8.2 %copy-start.9 = (f32[3,256]{1,0:T(4,128)S(1)}, f32[3,256]{1,0:T(4,128)}, u32[]{:S(2)}) copy-start(f32[3,256]{1,0:T(4,128)} %taps.3) | copy-start | bytes 9220
  108.9 8.2 %collective-permute-start.26 = (bf16[512,256]{1,0:T(8,128)(2,1)S(1)}, bf16[512,256]{1,0:T(8,128)(2,1)S(1)}, u32[]{:S(2)}, u32[]{:S(2)}) collective-permute-start(bf16[512,256]{1,0:T(8,128)(2,1)S(1)} %add_convert_fusion), channel_id=1, source_target_pairs={{0,2},{2,0},{1,3},{3,1},{4,6},{6,4},{5,7},{7,5},{8,10},{10,8},{9,1... | collective-permute-start | bytes 786440 | tf_op jit(solution)/shard_map/ppermute | solution.py:349
  117.1 10.9 %copy-start.10 = (f32[256]{0:T(256)S(1)}, f32[256]{0:T(256)}, u32[]{:S(2)}) copy-start(f32[256]{0:T(256)} %param.21) | copy-start | bytes 3076
  119.5 3.8 %collective-permute-start.27 = (f32[24,256]{1,0:T(8,128)S(1)}, f32[24,256]{1,0:T(8,128)S(1)}, u32[]{:S(2)}, u32[]{:S(2)}) collective-permute-start(f32[24,256]{1,0:T(8,128)S(1)} %get-tuple-element.78), channel_id=1, source_target_pairs={{0,32},{32,0},{1,33},{33,1},{2,34},{34,2},{3,35},{35,3},{4,36},{36... | collective-permute-start | bytes 73736 | tf_op jit(solution)/shard_map/ppermute | solution.py:349
  123.4 7.2 %collective-permute-start.28 = (f32[2,24,256]{2,1,0:T(8,128)S(1)}, f32[2,24,256]{2,1,0:T(8,128)S(1)}, u32[]{:S(2)}, u32[]{:S(2)}) collective-permute-start(f32[2,24,256]{2,1,0:T(8,128)S(1)} %pad_maximum_fusion.2.g0), channel_id=1, source_target_pairs={{0,64},{64,128},{128,192},{192,0},{1,65},{65,129},{129,193},{193,1... | collective-permute-start | bytes 147464 | tf_op jit(solution)/shard_map/ppermute | solution.py:349
  124.5 6.0 %collective-permute-start.29 = (f32[2,24,256]{2,1,0:T(8,128)S(1)}, f32[2,24,256]{2,1,0:T(8,128)S(1)}, u32[]{:S(2)}, u32[]{:S(2)}) collective-permute-start(f32[2,24,256]{2,1,0:T(8,128)S(1)} %pad_maximum_fusion.2.g0), channel_id=1, source_target_pairs={{0,128},{64,192},{128,0},{192,64},{1,129},{65,193},{129,1},{193,65... | collective-permute-start | bytes 147464 | tf_op jit(solution)/shard_map/ppermute | solution.py:349
  127.6 4.1 %collective-permute-start.30 = (f32[2,24,256]{2,1,0:T(8,128)S(1)}, f32[2,24,256]{2,1,0:T(8,128)S(1)}, u32[]{:S(2)}, u32[]{:S(2)}) collective-permute-start(f32[2,24,256]{2,1,0:T(8,128)S(1)} %pad_maximum_fusion.2.g0), channel_id=1, source_target_pairs={{0,192},{64,0},{128,64},{192,128},{1,193},{65,1},{129,65},{193,129... | collective-permute-start | bytes 147464 | tf_op jit(solution)/shard_map/ppermute | solution.py:349
  128.0 3.7 %copy-start.6 = (bf16[512,256]{1,0:T(8,128)(2,1)S(1)}, bf16[512,256]{1,0:T(8,128)(2,1)}, u32[]{:S(2)}) copy-start(bf16[512,256]{1,0:T(8,128)(2,1)} %gate.3) | copy-start | bytes 786436
where the time goes:
time: 134 us; the launch traced here: 133 us
  waiting for transfers between devices  64 us (48%)
  starting transfers between devices  43.1 us (32%)
  Pallas kernels  21.6 us (16%)
  local copies, waits for them, and re-layouts  2.92 us (2%)
    ppermute x27, waiting for transfers between devices, shift(): lax.ppermute(value, axis, [(i, (i + by) % count) for i in range(count)])  57.6 us
    ppermute x27, starting transfers between devices, shift(): lax.ppermute(value, axis, [(i, (i + by) % count) for i in range(count)])  37 us
    pallas_call x10, Pallas kernels, call(): pl.pallas_call(kernel, out_shape=out, in_specs=[pl.BlockSpec(memory_space...  21.6 us
    ppermute x4, waiting for transfers between devices, per_device(): lax.ppermute(packed[a], ('x', 'c'), head_route(a))  6.41 us
    ppermute x4, starting transfers between devices, per_device(): lax.ppermute(packed[a], ('x', 'c'), head_route(a))  6.09 us
    unnamed x22, local copies, waits for them, and re-layouts  2.88 us
  transfers between devices with their start and end apart: 31, of which 17 were waited for; matrix products, arithmetic and copies ran while one was open for 1% of the time, Pallas kernels for 7%

commit v1 on v0

--- a/solution.py
+++ b/solution.py
@@ -22,6 +22,10 @@
 
 def near_core(value):
     return pltpu.with_memory_space_constraint(value, pltpu.VMEM)
+
+
+def far_core(value):
+    return pltpu.with_memory_space_constraint(value, pltpu.HBM)
 
 
 def local_call(kernel, out_shape, mib, scratch_shapes=(), micros=2, near=True, big=()):
@@ -39,7 +43,7 @@
             scratch_shapes=scratch_shapes,
             cost_estimate=cost,
             compiler_params=vmem_params(mib),
-        )(*[near_core(o) if near else o for o in operands])
+        )(*[near_core(o) if near else far_core(o) for o in operands])
 
     return call
 
@@ -106,8 +110,17 @@
     def order(k_src, v_src):
         for xs in range(4):
             low = x0 ^ (xs & 1)
-            k_s[xs] = k_src[2 * (xs >> 1) + low]
-            v_s[xs] = v_src[2 * (1 ^ (xs >> 1)) + low]
+            k_high, v_high = (xs >> 1, 1 ^ (xs >> 1))
+
+            @pl.when(low == 1)
+            def _(xs=xs, k_high=k_high, v_high=v_high):
+                k_s[xs] = k_src[0][k_high]
+                v_s[xs] = v_src[0][v_high]
+
+            @pl.when(low == 0)
+            def _(xs=xs, k_high=k_high, v_high=v_high):
+                k_s[xs] = k_src[1][k_high]
+                v_s[xs] = v_src[1][v_high]
 
     @pl.when(c == 0)
     def _():
@@ -118,69 +131,81 @@
         order(other, mine)
 
 
-def near_kernel(r0, r1, r2, r3, mine, other, q_s, acc_ref, tot_ref, top_ref, k_s, v_s, s_s):
+def weigh(s_s, v_s, top, segments, slot, total, acc):
+    for s in segments:
+        p = jnp.exp2((s_s[slot + s] - top) * FACTOR)
+        total = total + lanes(jnp.add, p)
+        acc = acc + dot(p.astype(jnp.bfloat16), v_s[s])
+    return (total, acc)
+
+
+def near_kernel(
+    r0, r1, r2, r3, m1, m0, t1, t0, q_s, acc_ref, tot_ref, top_ref, k_s, v_s, s_s
+):
     x = lax.axis_index("x")
     c = lax.axis_index("c")
-    keys = mine.shape[1]
+    keys = m1.shape[1]
     rows = q_s.shape[1]
     for a, ref in enumerate((r0, r1, r2, r3)):
         q_s[2 * (c ^ (a >> 1)) + ((x & 1) ^ (a & 1))] = ref[keys:, :]
-    order_heads(mine, other, k_s, v_s)
-    for d in range(4):
-        xs = (x + d) & 3
+    order_heads((m1, m0), (t1, t0), k_s, v_s)
+    row = lax.broadcasted_iota(jnp.int32, (rows, keys), 0) + c * rows
+    col = lax.broadcasted_iota(jnp.int32, (rows, keys), 1)
+    zero = jnp.zeros((rows, HD), jnp.float32)
+    for xs in range(4):
+        slot = xs * (xs + 1) // 2
         query = q_s[xs]
-
-        def first(s, top, query=query):
+        top = None
+        for s in range(xs + 1):
             sc = scores_of(query, k_s[s])
-            s_s[s] = sc
-            return jnp.maximum(top, lanes(jnp.maximum, sc))
-
-        sc = scores_of(query, k_s[xs])
-        row = lax.broadcasted_iota(jnp.int32, (rows, keys), 0) + c * rows
-        col = lax.broadcasted_iota(jnp.int32, (rows, keys), 1)
-        sc = jnp.where(col <= row, sc, masked_floor)
-        s_s[xs] = sc
-        top = lax.fori_loop(0, xs, first, lanes(jnp.maximum, sc))
+            if s == xs:
+                sc = jnp.where(col <= row, sc, masked_floor)
+            s_s[slot + s] = sc
+            here = lanes(jnp.maximum, sc)
+            top = here if top is None else jnp.maximum(top, here)
         top = jnp.max(top, axis=1, keepdims=True)
-
-        def second(s, carry, top=top):
-            total, acc = carry
-            p = jnp.exp2((s_s[s] - top) * FACTOR)
-            return (total + lanes(jnp.add, p), acc + dot(p.astype(jnp.bfloat16), v_s[s]))
-
-        zero = jnp.zeros((rows, HD), jnp.float32)
-        total, acc = lax.fori_loop(0, xs + 1, second, (zero, zero))
-        acc_ref[d] = acc
-        tot_ref[d] = total
-        top_ref[d] = jnp.broadcast_to(top, (rows, HD))
-
-
-def far_kernel(q_s, acc_ref, tot_ref, top_ref, mine, other, o0, o1, o2, o3, k_s, v_s, s_s):
+        total, acc = weigh(s_s, v_s, top, range(xs + 1), slot, zero, zero)
+        acc_ref[xs] = acc
+        tot_ref[xs] = total
+        top_ref[xs] = jnp.broadcast_to(top, (rows, HD))
+
+
+def far_kernel(
+    q_s, acc_ref, tot_ref, top_ref, m1, m0, t1, t0, o0, o1, o2, o3, k_s, v_s, s_s, out_s
+):
     x = lax.axis_index("x")
     yl = lax.axis_index("yl")
-    order_heads(mine, other, k_s, v_s)
+    order_heads((m1, m0), (t1, t0), k_s, v_s)
+
+    def run(late):
+        for xs in range(4):
+            segments = range(xs + late)
+            slot = xs * (xs + 1) // 2
+            query = q_s[xs]
+            old = top_ref[xs]
+            top = old
+            for s in segments:
+                sc = scores_of(query, k_s[s])
+                s_s[slot + s] = sc
+                top = jnp.maximum(top, lanes(jnp.maximum, sc))
+            top = jnp.max(top, axis=1, keepdims=True)
+            fade = jnp.exp2((old - top) * FACTOR)
+            total, acc = weigh(
+                s_s, v_s, top, segments, slot, tot_ref[xs] * fade, acc_ref[xs] * fade
+            )
+            total = jnp.sum(total, axis=1, keepdims=True)
+            out_s[xs] = (acc / total).astype(jnp.bfloat16)
+
+    @pl.when(yl == 0)
+    def _():
+        run(0)
+
+    @pl.when(yl == 1)
+    def _():
+        run(1)
+
     for d, out in enumerate((o0, o1, o2, o3)):
-        xs = (x + d) & 3
-        query = q_s[xs]
-
-        def first(s, top, query=query):
-            sc = scores_of(query, k_s[s])
-            s_s[s] = sc
-            return jnp.maximum(top, lanes(jnp.maximum, sc))
-
-        old = top_ref[d]
-        top = lax.fori_loop(0, xs + yl, first, old)
-        top = jnp.max(top, axis=1, keepdims=True)
-
-        def second(s, carry, top=top):
-            total, acc = carry
-            p = jnp.exp2((s_s[s] - top) * FACTOR)
-            return (total + lanes(jnp.add, p), acc + dot(p.astype(jnp.bfloat16), v_s[s]))
-
-        fade = jnp.exp2((old - top) * FACTOR)
-        total, acc = lax.fori_loop(0, xs + yl, second, (tot_ref[d] * fade, acc_ref[d] * fade))
-        total = jnp.sum(total, axis=1, keepdims=True)
-        out[...] = (acc / total).astype(jnp.bfloat16)
+        out[...] = out_s[(x + d) & 3]
 
 
 def weight_pick_kernel(w_ref, keep, send):
@@ -369,18 +394,23 @@
     skip = skip_gain.reshape(1, width)
 
     packed = local_call(pack_kernel, [struct((rows + half, HD), bf16)] * 4, 4, near=False)(query_rows, key_rows, value_rows)
-    came = [lax.ppermute(packed[a], ("x", "c"), head_route(a)) for a in range(4)]
-    own_m = jnp.stack([piece[:rows] for piece in came])
-    far_m = shift(own_m, "yl", NYL, 1)
-    own_x = shift(own_m, "c", NC, 1)
-    kv = [pltpu.VMEM((4, rows, HD), bf16)] * 2 + [pltpu.VMEM((4, half, rows), f32)]
+    came = [None] * 4
+    for a in (1, 3, 0, 2):
+        came[a] = lax.ppermute(packed[a], ("x", "c"), head_route(a))
+    odd_m = jnp.stack([came[1][:rows], came[3][:rows]])
+    even_m = jnp.stack([came[0][:rows], came[2][:rows]])
+    odd_far = shift(odd_m, "yl", NYL, 1)
+    even_far = shift(even_m, "yl", NYL, 1)
+    odd_x = shift(odd_m, "c", NC, 1)
+    even_x = shift(even_m, "c", NC, 1)
+    kv = [pltpu.VMEM((4, rows, HD), bf16)] * 2 + [pltpu.VMEM((10, half, rows), f32)]
     near = local_call(
         near_kernel,
         [struct((4, half, HD), bf16)] + [struct((4, half, HD), f32)] * 3,
-        6,
+        12,
         kv,
-        micros=6,
-    )(*came, own_m, own_x)
+        micros=4,
+    )(*came, odd_m, even_m, odd_x, even_x)
 
     k_rows = out_weight.shape[0]
     w_keep, w_send = local_call(
@@ -393,8 +423,15 @@
         2,
     )(decay_rates, residues)
 
-    far_x = shift(tie(far_m, near[3]), "c", NC, 1)
-    heads = local_call(far_kernel, [struct((half, HD), bf16)] * 4, 6, kv, micros=6)(*near, far_m, far_x)
+    odd_far_x = shift(odd_far, "c", NC, 1)
+    even_far_x = shift(tie(even_far, near[3]), "c", NC, 1)
+    heads = local_call(
+        far_kernel,
+        [struct((half, HD), bf16)] * 4,
+        12,
+        kv + [pltpu.VMEM((4, half, HD), bf16)],
+        micros=4,
+    )(*near, odd_far, even_far, odd_far_x, even_far_x)
     hm = jnp.stack([heads[0]] + [shift(heads[d], "x", NX, d) for d in range(1, 4)])
     ho = shift(hm, "c", NC, 1)
 

time: 134 us -> 126 us (0.940)
  waiting for transfers between devices: 64 us -> 57.1 us
  starting transfers between devices: 43.1 us -> 49.9 us
  Pallas kernels: 21.6 us -> 16.4 us
  local copies, waits for them, and re-layouts: 2.92 us -> 0.08 us
    ppermute x27 -> x30, starting transfers between devices: 37 us -> 43.8 us  [shift(): lax.ppermute(value, axis, [(i, (i + by) % count) for i in range(count)])]
    pallas_call x10, Pallas kernels: 21.6 us -> 16.4 us  [call(): pl.pallas_call(kernel, out_shape=out, in_specs=[pl.BlockSpec(memory_space...]
    ppermute x4, waiting for transfers between devices: 6.41 us -> 1.46 us  [per_device(): came[a] = lax.ppermute(packed[a], ('x', 'c'), head_route(a))]
    unnamed x22 -> x16, local copies, waits for them, and re-layouts: 2.88 us -> 0.04 us
    ppermute x27 -> x30, waiting for transfers between devices: 57.6 us -> 55.7 us  [shift(): lax.ppermute(value, axis, [(i, (i + by) % count) for i in range(count)])]
  transfers between devices with their start and end apart: 31 -> 34, of which waited for: 17 -> 20; matrix products, arithmetic and copies ran while one was open for 1% -> 1% of each run, Pallas kernels for 7% -> 5%
where the time goes in v1:
time: 126 us; the launch traced here: 125 us
  waiting for transfers between devices  57.1 us (45%)
  starting transfers between devices  49.9 us (40%)
  Pallas kernels  16.4 us (13%)
    ppermute x30, waiting for transfers between devices, shift(): lax.ppermute(value, axis, [(i, (i + by) % count) for i in range(count)])  55.7 us
    ppermute x30, starting transfers between devices, shift(): lax.ppermute(value, axis, [(i, (i + by) % count) for i in range(count)])  43.8 us
    pallas_call x10, Pallas kernels, call(): pl.pallas_call(kernel, out_shape=out, in_specs=[pl.BlockSpec(memory_space...  16.4 us
    ppermute x4, starting transfers between devices, per_device(): came[a] = lax.ppermute(packed[a], ('x', 'c'), head_route(a))  6.09 us
  transfers between devices with their start and end apart: 34, of which 20 were waited for; matrix products, arithmetic and copies ran while one was open for 1% of the time, Pallas kernels for 5%

profile of v1, /device:TPU:26, one launch (start us, length us, event | category | flops | bytes accessed | tf_op | source)
XLA Modules:
  0.0 125.4 jit_solution(10672000495069277403)
XLA Ops:
  0.6 1.3 %shard_map.122 = (bf16[768,128]{1,0:T(8,128)(2,1)S(1)}, bf16[768,128]{1,0:T(8,128)(2,1)S(1)}, bf16[768,128]{1,0:T(8,128)(2,1)S(1)}, bf16[768,128]{1,0:T(8,128)(2,1)S(1)}) custom-call(bf16[512,256]{1,0:T(8,128)(2,1)} %q_ref.1, bf16[512,256]{1,0:T(8,128)(2,1)} %k_ref.1, bf16[512,256]{1,0:T(8,128)(2,1)} %v_ref.1), custom_call_target="tpu_custom_call" | custom-call | flops 2000000000 | bytes 6000000 | tf_op jit(solution)/shard_map/pallas_call | solution.py:38
  1.9 0.1 collective-permute-start.3
  2.0 0.7 collective-permute-start
  2.7 1.5 %collective-permute-start.1 = (bf16[768,128]{1,0:T(8,128)(2,1)S(1)}, bf16[768,128]{1,0:T(8,128)(2,1)S(1)}, u32[]{:S(2)}, u32[]{:S(2)}) collective-permute-start(bf16[768,128]{1,0:T(8,128)(2,1)S(1)} %get-tuple-element.42), channel_id=1, source_target_pairs={{0,64},{1,192},{64,0},{65,128},{128,65},{129,193},{192,1},{193,129... | collective-permute-start | bytes 589832 | tf_op jit(solution)/shard_map/ppermute | solution.py:399
  4.2 3.8 %collective-permute-start.2 = (bf16[768,128]{1,0:T(8,128)(2,1)S(1)}, bf16[768,128]{1,0:T(8,128)(2,1)S(1)}, u32[]{:S(2)}, u32[]{:S(2)}) collective-permute-start(bf16[768,128]{1,0:T(8,128)(2,1)S(1)} %get-tuple-element.43), channel_id=1, source_target_pairs={{0,1},{1,129},{64,65},{65,193},{128,0},{129,128},{192,64},{193,192... | collective-permute-start | bytes 589832 | tf_op jit(solution)/shard_map/ppermute | solution.py:399
  8.0 1.5 %collective-permute-done.1.r1 = bf16[768,128]{1,0:T(8,128)(2,1)S(1)} collective-permute-done((bf16[768,128]{1,0:T(8,128)(2,1)S(1)}, bf16[768,128]{1,0:T(8,128)(2,1)S(1)}, u32[]{:S(2)}, u32[]{:S(2)}) %collective-permute-start.1) | collective-permute-done | bytes 196640 | tf_op jit(solution)/shard_map/ppermute | solution.py:399
  9.5 6.5 %collective-permute-start.4 = (bf16[2,512,128]{2,1,0:T(8,128)(2,1)S(1)}, bf16[2,512,128]{2,1,0:T(8,128)(2,1)S(1)}, u32[]{:S(2)}, u32[]{:S(2)}) collective-permute-start(bf16[2,512,128]{2,1,0:T(8,128)(2,1)S(1)} %pad_maximum_fusion.m1), channel_id=1, source_target_pairs={{0,1},{1,0},{2,3},{3,2},{4,5},{5,4},{6,7},{7,6},{8,9},{9,8},{10,11... | collective-permute-start | bytes 786440 | tf_op jit(solution)/shard_map/ppermute | solution.py:374
  16.1 0.1 collective-permute-start.5
  16.2 1.0 collective-permute-done.4.t1
  17.2 0.6 collective-permute-done.5.t0
  17.7 2.4 %shard_map.123 = (bf16[4,256,128]{2,1,0:T(8,128)(2,1)S(1)}, f32[4,256,128]{2,1,0:T(8,128)S(1)}, f32[4,256,128]{2,1,0:T(8,128)S(1)}, f32[4,256,128]{2,1,0:T(8,128)S(1)}) custom-call(bf16[768,128]{1,0:T(8,128)(2,1)S(1)} %collective-permute-done.r0, bf16[768,128]{1,0:T(8,128)(2,1)S(1)} %collective-permute-done.1.r1, ...), custom_call_target="tpu_custom_call" | custom-call | flops 4000000000 | bytes 12000000 | tf_op jit(solution)/shard_map/pallas_call | solution.py:38
  20.2 0.6 shard_map.125
  20.7 0.3 collective-permute-start.14
  21.0 0.7 collective-permute-start.7
  21.8 1.3 %collective-permute-start.6 = (bf16[2,512,128]{2,1,0:T(8,128)(2,1)S(1)}, bf16[2,512,128]{2,1,0:T(8,128)(2,1)S(1)}, u32[]{:S(2)}, u32[]{:S(2)}) collective-permute-start(bf16[2,512,128]{2,1,0:T(8,128)(2,1)S(1)} %pad_maximum_fusion.m1), channel_id=1, source_target_pairs={{0,32},{32,0},{1,33},{33,1},{2,34},{34,2},{3,35},{35,3},{4,36},{36... | collective-permute-start | bytes 786440 | tf_op jit(solution)/shard_map/ppermute | solution.py:374
  23.0 7.2 %collective-permute-done.7.m0 = bf16[2,512,128]{2,1,0:T(8,128)(2,1)S(1)} collective-permute-done((bf16[2,512,128]{2,1,0:T(8,128)(2,1)S(1)}, bf16[2,512,128]{2,1,0:T(8,128)(2,1)S(1)}, u32[]{:S(2)}, u32[]{:S(2)}) %collective-permute-start.7) | collective-permute-done | bytes 262176 | tf_op jit(solution)/shard_map/ppermute | solution.py:374
  30.2 5.0 %collective-permute-done.6.m1 = bf16[2,512,128]{2,1,0:T(8,128)(2,1)S(1)} collective-permute-done((bf16[2,512,128]{2,1,0:T(8,128)(2,1)S(1)}, bf16[2,512,128]{2,1,0:T(8,128)(2,1)S(1)}, u32[]{:S(2)}, u32[]{:S(2)}) %collective-permute-start.6) | collective-permute-done | bytes 262176 | tf_op jit(solution)/shard_map/ppermute | solution.py:374
  35.2 0.5 collective-permute-start.9
  35.7 1.0 collective-permute-done.8.t1
  36.7 0.4 collective-permute-done.9.t0
  37.1 2.8 %shard_map.124 = (bf16[256,128]{1,0:T(8,128)(2,1)S(1)}, bf16[256,128]{1,0:T(8,128)(2,1)S(1)}, bf16[256,128]{1,0:T(8,128)(2,1)S(1)}, bf16[256,128]{1,0:T(8,128)(2,1)S(1)}) custom-call(bf16[4,256,128]{2,1,0:T(8,128)(2,1)S(1)} %get-tuple-element.45.q_s, f32[4,256,128]{2,1,0:T(8,128)S(1)} %get-tuple-element.46.acc_ref, ...), custom_call_target="tpu_custom_call" | custom-call | flops 4000000000 | bytes 12000000 | tf_op jit(solution)/shard_map/pallas_call | solution.py:38
  39.9 2.3 %collective-permute-start.12 = (bf16[256,128]{1,0:T(8,128)(2,1)S(1)}, bf16[256,128]{1,0:T(8,128)(2,1)S(1)}, u32[]{:S(2)}, u32[]{:S(2)}) collective-permute-start(bf16[256,128]{1,0:T(8,128)(2,1)S(1)} %get-tuple-element.53), channel_id=1, source_target_pairs={{0,192},{64,0},{128,64},{192,128},{1,193},{65,1},{129,65},{193,129... | collective-permute-start | bytes 196616 | tf_op jit(solution)/shard_map/ppermute | solution.py:374
  42.2 0.6 collective-permute-start.11
  42.7 1.9 %collective-permute-start.10 = (bf16[256,128]{1,0:T(8,128)(2,1)S(1)}, bf16[256,128]{1,0:T(8,128)(2,1)S(1)}, u32[]{:S(2)}, u32[]{:S(2)}) collective-permute-start(bf16[256,128]{1,0:T(8,128)(2,1)S(1)} %get-tuple-element.51), channel_id=1, source_target_pairs={{0,64},{64,128},{128,192},{192,0},{1,65},{65,129},{129,193},{193,1... | collective-permute-start | bytes 196616 | tf_op jit(solution)/shard_map/ppermute | solution.py:374
  44.7 3.3 %collective-permute-done.11 = bf16[256,128]{1,0:T(8,128)(2,1)S(1)} collective-permute-done((bf16[256,128]{1,0:T(8,128)(2,1)S(1)}, bf16[256,128]{1,0:T(8,128)(2,1)S(1)}, u32[]{:S(2)}, u32[]{:S(2)}) %collective-permute-start.11) | collective-permute-done | bytes 65568 | tf_op jit(solution)/shard_map/ppermute | solution.py:374
  48.0 0.1 collective-permute-start.13
  48.1 1.5 %collective-permute-done.13.ho = bf16[4,256,128]{2,1,0:T(8,128)(2,1)S(1)} collective-permute-done((bf16[4,256,128]{2,1,0:T(8,128)(2,1)S(1)}, bf16[4,256,128]{2,1,0:T(8,128)(2,1)S(1)}, u32[]{:S(2)}, u32[]{:S(2)}) %collective-permute-start.13) | collective-permute-done | bytes 262176 | tf_op jit(solution)/shard_map/ppermute | solution.py:374
  49.6 2.1 %shard_map.126 = (bf16[512,256]{1,0:T(8,128)(2,1)S(1)}, bf16[512,256]{1,0:T(8,128)(2,1)S(1)}, bf16[512,256]{1,0:T(8,128)(2,1)S(1)}, bf16[512,256]{1,0:T(8,128)(2...) custom-call(bf16[4,256,128]{2,1,0:T(8,128)(2,1)S(1)} %pad_maximum_fu, ...), custom_call_target="tpu_custom_call" | custom-call | flops 7000000000 | bytes 21000000 | tf_op jit(solution)/shard_map/pallas_call | solution.py:38
  51.8 2.0 %collective-permute-start.15 = (bf16[512,256]{1,0:T(8,128)(2,1)S(1)}, bf16[512,256]{1,0:T(8,128)(2,1)S(1)}, u32[]{:S(2)}, u32[]{:S(2)}) collective-permute-start(bf16[512,256]{1,0:T(8,128)(2,1)S(1)} %get-tuple-element.58), channel_id=1, source_target_pairs={{0,4},{4,8},{8,12},{12,16},{16,20},{20,24},{24,28},{28,0},{1,5},{5... | collective-permute-start | bytes 786440 | tf_op jit(solution)/shard_map/ppermute | solution.py:374
  53.7 0.5 shard_map.127
  54.3 2.0 %collective-permute-start.22 = (bf16[512,256]{1,0:T(8,128)(2,1)S(1)}, bf16[512,256]{1,0:T(8,128)(2,1)S(1)}, u32[]{:S(2)}, u32[]{:S(2)}) collective-permute-start(bf16[512,256]{1,0:T(8,128)(2,1)S(1)} %get-tuple-element.66), channel_id=1, source_target_pairs={{0,4},{4,8},{8,12},{12,16},{16,20},{20,24},{24,28},{28,0},{1,5},{5... | collective-permute-start | bytes 786440 | tf_op jit(solution)/shard_map/ppermute | solution.py:374
  56.3 2.1 %collective-permute-start.18 = (bf16[512,256]{1,0:T(8,128)(2,1)S(1)}, bf16[512,256]{1,0:T(8,128)(2,1)S(1)}, u32[]{:S(2)}, u32[]{:S(2)}) collective-permute-start(bf16[512,256]{1,0:T(8,128)(2,1)S(1)} %get-tuple-element.61), channel_id=1, source_target_pairs={{0,28},{4,0},{8,4},{12,8},{16,12},{20,16},{24,20},{28,24},{1,29},{... | collective-permute-start | bytes 786440 | tf_op jit(solution)/shard_map/ppermute | solution.py:374
  58.4 2.0 %collective-permute-start.26 = (bf16[512,256]{1,0:T(8,128)(2,1)S(1)}, bf16[512,256]{1,0:T(8,128)(2,1)S(1)}, u32[]{:S(2)}, u32[]{:S(2)}) collective-permute-start(bf16[512,256]{1,0:T(8,128)(2,1)S(1)} %get-tuple-element.70), channel_id=1, source_target_pairs={{0,28},{4,0},{8,4},{12,8},{16,12},{20,16},{24,20},{28,24},{1,29},{... | collective-permute-start | bytes 786440 | tf_op jit(solution)/shard_map/ppermute | solution.py:374
  60.4 4.5 %collective-permute-done.15 = bf16[512,256]{1,0:T(8,128)(2,1)S(1)} collective-permute-done((bf16[512,256]{1,0:T(8,128)(2,1)S(1)}, bf16[512,256]{1,0:T(8,128)(2,1)S(1)}, u32[]{:S(2)}, u32[]{:S(2)}) %collective-permute-start.15) | collective-permute-done | bytes 262176 | tf_op jit(solution)/shard_map/ppermute | solution.py:374
  64.9 0.1 collective-permute-start.16
  65.0 5.5 %collective-permute-done.22 = bf16[512,256]{1,0:T(8,128)(2,1)S(1)} collective-permute-done((bf16[512,256]{1,0:T(8,128)(2,1)S(1)}, bf16[512,256]{1,0:T(8,128)(2,1)S(1)}, u32[]{:S(2)}, u32[]{:S(2)}) %collective-permute-start.22) | collective-permute-done | bytes 262176 | tf_op jit(solution)/shard_map/ppermute | solution.py:374
  70.5 0.1 collective-permute-start.23
  70.7 3.5 %collective-permute-start.19 = (bf16[512,256]{1,0:T(8,128)(2,1)S(1)}, bf16[512,256]{1,0:T(8,128)(2,1)S(1)}, u32[]{:S(2)}, u32[]{:S(2)}) collective-permute-start(bf16[512,256]{1,0:T(8,128)(2,1)S(1)} %add_convert_fusion.8), channel_id=1, source_target_pairs={{0,28},{4,0},{8,4},{12,8},{16,12},{20,16},{24,20},{28,24},{1,29},{... | collective-permute-start | bytes 786440 | tf_op jit(solution)/shard_map/ppermute | solution.py:374
  74.3 0.9 collective-permute-start.27
  75.2 6.0 %collective-permute-done.23 = bf16[512,256]{1,0:T(8,128)(2,1)S(1)} collective-permute-done((bf16[512,256]{1,0:T(8,128)(2,1)S(1)}, bf16[512,256]{1,0:T(8,128)(2,1)S(1)}, u32[]{:S(2)}, u32[]{:S(2)}) %collective-permute-start.23) | collective-permute-done | bytes 262176 | tf_op jit(solution)/shard_map/ppermute | solution.py:374
  81.2 0.1 collective-permute-start.24
  81.4 3.4 %collective-permute-start.20 = (bf16[512,256]{1,0:T(8,128)(2,1)S(1)}, bf16[512,256]{1,0:T(8,128)(2,1)S(1)}, u32[]{:S(2)}, u32[]{:S(2)}) collective-permute-start(bf16[512,256]{1,0:T(8,128)(2,1)S(1)} %add_convert_fusion.7), channel_id=1, source_target_pairs={{0,28},{4,0},{8,4},{12,8},{16,12},{20,16},{24,20},{28,24},{1,29},{... | collective-permute-start | bytes 786440 | tf_op jit(solution)/shard_map/ppermute | solution.py:374
  84.8 3.5 %collective-permute-start.28 = (bf16[512,256]{1,0:T(8,128)(2,1)S(1)}, bf16[512,256]{1,0:T(8,128)(2,1)S(1)}, u32[]{:S(2)}, u32[]{:S(2)}) collective-permute-start(bf16[512,256]{1,0:T(8,128)(2,1)S(1)} %add_convert_fusion.1), channel_id=1, source_target_pairs={{0,28},{4,0},{8,4},{12,8},{16,12},{20,16},{24,20},{28,24},{1,29},{... | collective-permute-start | bytes 786440 | tf_op jit(solution)/shard_map/ppermute | solution.py:374
  88.4 1.9 %collective-permute-done.24 = bf16[512,256]{1,0:T(8,128)(2,1)S(1)} collective-permute-done((bf16[512,256]{1,0:T(8,128)(2,1)S(1)}, bf16[512,256]{1,0:T(8,128)(2,1)S(1)}, u32[]{:S(2)}, u32[]{:S(2)}) %collective-permute-start.24) | collective-permute-done | bytes 262176 | tf_op jit(solution)/shard_map/ppermute | solution.py:374
  90.3 0.1 collective-permute-start.25
  90.5 0.1 collective-permute-start.17
  90.6 0.8 collective-permute-done.20
  91.4 0.1 add_convert_fusion.6
  91.5 3.8 %collective-permute-start.21 = (bf16[512,256]{1,0:T(8,128)(2,1)S(1)}, bf16[512,256]{1,0:T(8,128)(2,1)S(1)}, u32[]{:S(2)}, u32[]{:S(2)}) collective-permute-start(bf16[512,256]{1,0:T(8,128)(2,1)S(1)} %add_convert_fusion.6), channel_id=1, source_target_pairs={{0,28},{4,0},{8,4},{12,8},{16,12},{20,16},{24,20},{28,24},{1,29},{... | collective-permute-start | bytes 786440 | tf_op jit(solution)/shard_map/ppermute | solution.py:374
  95.3 1.8 %collective-permute-done.28 = bf16[512,256]{1,0:T(8,128)(2,1)S(1)} collective-permute-done((bf16[512,256]{1,0:T(8,128)(2,1)S(1)}, bf16[512,256]{1,0:T(8,128)(2,1)S(1)}, u32[]{:S(2)}, u32[]{:S(2)}) %collective-permute-start.28) | collective-permute-done | bytes 262176 | tf_op jit(solution)/shard_map/ppermute | solution.py:374
  97.1 3.8 %collective-permute-done.25 = bf16[512,256]{1,0:T(8,128)(2,1)S(1)} collective-permute-done((bf16[512,256]{1,0:T(8,128)(2,1)S(1)}, bf16[512,256]{1,0:T(8,128)(2,1)S(1)}, u32[]{:S(2)}, u32[]{:S(2)}) %collective-permute-start.25) | collective-permute-done | bytes 262176 | tf_op jit(solution)/shard_map/ppermute | solution.py:374
  100.8 0.1 add_convert_fusion
  101.0 1.3 %collective-permute-start.29 = (bf16[512,256]{1,0:T(8,128)(2,1)S(1)}, bf16[512,256]{1,0:T(8,128)(2,1)S(1)}, u32[]{:S(2)}, u32[]{:S(2)}) collective-permute-start(bf16[512,256]{1,0:T(8,128)(2,1)S(1)} %add_convert_fusion), channel_id=1, source_target_pairs={{0,2},{2,0},{1,3},{3,1},{4,6},{6,4},{5,7},{7,5},{8,10},{10,8},{9,1... | collective-permute-start | bytes 786440 | tf_op jit(solution)/shard_map/ppermute | solution.py:374
  102.3 0.1 shard_map.128
  102.4 1.7 %collective-permute-done.17.plus = bf16[512,256]{1,0:T(8,128)(2,1)S(1)} collective-permute-done((bf16[512,256]{1,0:T(8,128)(2,1)S(1)}, bf16[512,256]{1,0:T(8,128)(2,1)S(1)}, u32[]{:S(2)}, u32[]{:S(2)}) %collective-permute-start.17) | collective-permute-done | bytes 262176 | tf_op jit(solution)/shard_map/ppermute | solution.py:374
  104.2 5.0 %collective-permute-done.29.side = bf16[512,256]{1,0:T(8,128)(2,1)S(1)} collective-permute-done((bf16[512,256]{1,0:T(8,128)(2,1)S(1)}, bf16[512,256]{1,0:T(8,128)(2,1)S(1)}, u32[]{:S(2)}, u32[]{:S(2)}) %collective-permute-start.29) | collective-permute-done | bytes 262176 | tf_op jit(solution)/shard_map/ppermute | solution.py:374
  109.2 2.4 %shard_map.129 = (bf16[512,256]{1,0:T(8,128)(2,1)}, f32[512,256]{1,0:T(8,128)S(1)}, f32[16,16,256]{2,1,0:T(8,128)S(1)}, f32[24,256]{1,0:T(8,128)S(1)}) custom-call(bf16[512,256]{1,0:T(8,128)(2,1)S(1)} %get-tuple-element.57.own, bf16[512,256]{1,0:T(8,128)(2,1)S(1)} %collective-permute-done.17.plus, bf16[512,256]{1,0:T(8,128)(2,1)S(1)} %collective-permute-done.21.minus, ...), custom_call_target="tpu_custom_call" | custom-call | flops 2000000000 | bytes 6000000 | tf_op jit(solution)/shard_map/pallas_call | solution.py:38
  111.6 3.8 %collective-permute-done.30 = f32[24,256]{1,0:T(8,128)S(1)} collective-permute-done((f32[24,256]{1,0:T(8,128)S(1)}, f32[24,256]{1,0:T(8,128)S(1)}, u32[]{:S(2)}, u32[]{:S(2)}) %collective-permute-start.30) | collective-permute-done | bytes 24608 | tf_op jit(solution)/shard_map/ppermute | solution.py:374
  115.5 1.0 collective-permute-start.31
  116.5 3.1 %collective-permute-start.32 = (f32[2,24,256]{2,1,0:T(8,128)S(1)}, f32[2,24,256]{2,1,0:T(8,128)S(1)}, u32[]{:S(2)}, u32[]{:S(2)}) collective-permute-start(f32[2,24,256]{2,1,0:T(8,128)S(1)} %pad_maximum_fusion.3.g0), channel_id=1, source_target_pairs={{0,128},{64,192},{128,0},{192,64},{1,129},{65,193},{129,1},{193,65... | collective-permute-start | bytes 147464 | tf_op jit(solution)/shard_map/ppermute | solution.py:374
  119.5 0.6 collective-permute-start.33
  120.1 2.4 %shard_map.130.local = f32[512,256]{1,0:T(8,128)S(1)} custom-call(f32[512,256]{1,0:T(8,128)S(1)} %get-tuple-element.75.sig, f32[32,256]{1,0:T(8,128)S(1)} %get-tuple-element.76.filt, f32[1,256]{1,0:T(1,128)S(1)} %bitcast.17), custom_call_target="tpu_custom_call" | custom-call | flops 6000000000 | bytes 18000000 | tf_op jit(solution)/shard_map/pallas_call | solution.py:38
  122.5 1.1 collective-permute-done.33.g3
  123.6 1.7 %shard_map.131 = bf16[512,256]{1,0:T(8,128)(2,1)} custom-call(f32[512,256]{1,0:T(8,128)S(1)} %shard_map.130.local, f32[16,16,256]{2,1,0:T(8,128)S(1)} %get-tuple-element.77.blocks, f32[2,24,256]{2,1,0:T(8,128)S(1)} %pad_maximum_fusion.3.g0, f32[2,24,256]{2,1,0:T(8,128)S(1)} %collective-permute-done.31.g1, f32[2,24,256]{2,1,0:T(8,128)S(1)} %collective-permute-done.32.g2, ...), custom_call_target="tpu_custom_call" | custom-call | flops 2000000000 | bytes 6000000 | tf_op jit(solution)/shard_map/pallas_call | solution.py:38
  (49 shorter events, 0.8 us)
Async XLA Ops:
  1.9 6.1 %collective-permute-start.3 = (bf16[768,128]{1,0:T(8,128)(2,1)S(1)}, bf16[768,128]{1,0:T(8,128)(2,1)S(1)}, u32[]{:S(2)}, u32[]{:S(2)}) collective-permute-start(bf16[768,128]{1,0:T(8,128)(2,1)S(1)} %get-tuple-element.44), channel_id=1, source_target_pairs={{0,65},{1,193},{64,1},{65,129},{128,64},{129,192},{192,0},{193,128... | collective-permute-start | bytes 589832 | tf_op jit(solution)/shard_map/ppermute | solution.py:399
  2.0 14.0 %collective-permute-start = (bf16[768,128]{1,0:T(8,128)(2,1)S(1)}, bf16[768,128]{1,0:T(8,128)(2,1)S(1)}, u32[]{:S(2)}, u32[]{:S(2)}) collective-permute-start(bf16[768,128]{1,0:T(8,128)(2,1)S(1)} %get-tuple-element.41), channel_id=1, source_target_pairs={{0,0},{1,128},{64,64},{65,192},{128,1},{129,129},{192,65},{193,193... | collective-permute-start | bytes 589832 | tf_op jit(solution)/shard_map/ppermute | solution.py:399
  2.7 6.8 %collective-permute-start.1 = (bf16[768,128]{1,0:T(8,128)(2,1)S(1)}, bf16[768,128]{1,0:T(8,128)(2,1)S(1)}, u32[]{:S(2)}, u32[]{:S(2)}) collective-permute-start(bf16[768,128]{1,0:T(8,128)(2,1)S(1)} %get-tuple-element.42), channel_id=1, source_target_pairs={{0,64},{1,192},{64,0},{65,128},{128,65},{129,193},{192,1},{193,129... | collective-permute-start | bytes 589832 | tf_op jit(solution)/shard_map/ppermute | solution.py:399
  4.2 11.8 %collective-permute-start.2 = (bf16[768,128]{1,0:T(8,128)(2,1)S(1)}, bf16[768,128]{1,0:T(8,128)(2,1)S(1)}, u32[]{:S(2)}, u32[]{:S(2)}) collective-permute-start(bf16[768,128]{1,0:T(8,128)(2,1)S(1)} %get-tuple-element.43), channel_id=1, source_target_pairs={{0,1},{1,129},{64,65},{65,193},{128,0},{129,128},{192,64},{193,192... | collective-permute-start | bytes 589832 | tf_op jit(solution)/shard_map/ppermute | solution.py:399
  9.5 7.6 %collective-permute-start.4 = (bf16[2,512,128]{2,1,0:T(8,128)(2,1)S(1)}, bf16[2,512,128]{2,1,0:T(8,128)(2,1)S(1)}, u32[]{:S(2)}, u32[]{:S(2)}) collective-permute-start(bf16[2,512,128]{2,1,0:T(8,128)(2,1)S(1)} %pad_maximum_fusion.m1), channel_id=1, source_target_pairs={{0,1},{1,0},{2,3},{3,2},{4,5},{5,4},{6,7},{7,6},{8,9},{9,8},{10,11... | collective-permute-start | bytes 786440 | tf_op jit(solution)/shard_map/ppermute | solution.py:374
  16.1 4.1 %copy-start = (bf16[256,8192]{1,0:T(8,128)(2,1)S(1)}, bf16[256,8192]{1,0:T(8,128)(2,1)}, u32[]{:S(2)}) copy-start(bf16[256,8192]{1,0:T(8,128)(2,1)} %w_ref) | copy-start | bytes 12582916
  16.1 1.6 %collective-permute-start.5 = (bf16[2,512,128]{2,1,0:T(8,128)(2,1)S(1)}, bf16[2,512,128]{2,1,0:T(8,128)(2,1)S(1)}, u32[]{:S(2)}, u32[]{:S(2)}) collective-permute-start(bf16[2,512,128]{2,1,0:T(8,128)(2,1)S(1)} %pad_maximum_fusion.1.m0), channel_id=1, source_target_pairs={{0,1},{1,0},{2,3},{3,2},{4,5},{5,4},{6,7},{7,6},{8,9},{9,8},{10,11... | collective-permute-start | bytes 786440 | tf_op jit(solution)/shard_map/ppermute | solution.py:374
  20.7 28.9 %collective-permute-start.14 = (bf16[16,256,256]{2,1,0:T(8,128)(2,1)S(1)}, bf16[16,256,256]{2,1,0:T(8,128)(2,1)S(1)}, u32[]{:S(2)}, u32[]{:S(2)}) collective-permute-start(bf16[16,256,256]{2,1,0:T(8,128)(2,1)S(1)} %get-tuple-element.56), channel_id=1, source_target_pairs={{0,1},{1,0},{2,3},{3,2},{4,5},{5,4},{6,7},{7,6},{8,9},{9,8},{10,11... | collective-permute-start | bytes 6291464 | tf_op jit(solution)/shard_map/ppermute | solution.py:374
  21.0 9.2 %collective-permute-start.7 = (bf16[2,512,128]{2,1,0:T(8,128)(2,1)S(1)}, bf16[2,512,128]{2,1,0:T(8,128)(2,1)S(1)}, u32[]{:S(2)}, u32[]{:S(2)}) collective-permute-start(bf16[2,512,128]{2,1,0:T(8,128)(2,1)S(1)} %pad_maximum_fusion.1.m0), channel_id=1, source_target_pairs={{0,32},{32,0},{1,33},{33,1},{2,34},{34,2},{3,35},{35,3},{4,36},{36... | collective-permute-start | bytes 786440 | tf_op jit(solution)/shard_map/ppermute | solution.py:374
  21.8 13.4 %collective-permute-start.6 = (bf16[2,512,128]{2,1,0:T(8,128)(2,1)S(1)}, bf16[2,512,128]{2,1,0:T(8,128)(2,1)S(1)}, u32[]{:S(2)}, u32[]{:S(2)}) collective-permute-start(bf16[2,512,128]{2,1,0:T(8,128)(2,1)S(1)} %pad_maximum_fusion.m1), channel_id=1, source_target_pairs={{0,32},{32,0},{1,33},{33,1},{2,34},{34,2},{3,35},{35,3},{4,36},{36... | collective-permute-start | bytes 786440 | tf_op jit(solution)/shard_map/ppermute | solution.py:374
  35.2 1.5 %collective-permute-start.8 = (bf16[2,512,128]{2,1,0:T(8,128)(2,1)S(1)}, bf16[2,512,128]{2,1,0:T(8,128)(2,1)S(1)}, u32[]{:S(2)}, u32[]{:S(2)}) collective-permute-start(bf16[2,512,128]{2,1,0:T(8,128)(2,1)S(1)} %collective-permute-done.6.m1), channel_id=1, source_target_pairs={{0,1},{1,0},{2,3},{3,2},{4,5},{5,4},{6,7},{7,6},{8,9},{9,8},{10,11... | collective-permute-start | bytes 786440 | tf_op jit(solution)/shard_map/ppermute | solution.py:374
  35.2 1.9 %collective-permute-start.9 = (bf16[2,512,128]{2,1,0:T(8,128)(2,1)S(1)}, bf16[2,512,128]{2,1,0:T(8,128)(2,1)S(1)}, u32[]{:S(2)}, u32[]{:S(2)}) collective-permute-start(bf16[2,512,128]{2,1,0:T(8,128)(2,1)S(1)} %collective-permute-done.7.m0), channel_id=1, source_target_pairs={{0,1},{1,0},{2,3},{3,2},{4,5},{5,4},{6,7},{7,6},{8,9},{9,8},{10,11... | collective-permute-start | bytes 786440 | tf_op jit(solution)/shard_map/ppermute | solution.py:374
  39.9 4.7 %collective-permute-start.12 = (bf16[256,128]{1,0:T(8,128)(2,1)S(1)}, bf16[256,128]{1,0:T(8,128)(2,1)S(1)}, u32[]{:S(2)}, u32[]{:S(2)}) collective-permute-start(bf16[256,128]{1,0:T(8,128)(2,1)S(1)} %get-tuple-element.53), channel_id=1, source_target_pairs={{0,192},{64,0},{128,64},{192,128},{1,193},{65,1},{129,65},{193,129... | collective-permute-start | bytes 196616 | tf_op jit(solution)/shard_map/ppermute | solution.py:374
  42.2 5.8 %collective-permute-start.11 = (bf16[256,128]{1,0:T(8,128)(2,1)S(1)}, bf16[256,128]{1,0:T(8,128)(2,1)S(1)}, u32[]{:S(2)}, u32[]{:S(2)}) collective-permute-start(bf16[256,128]{1,0:T(8,128)(2,1)S(1)} %get-tuple-element.52), channel_id=1, source_target_pairs={{0,128},{64,192},{128,0},{192,64},{1,129},{65,193},{129,1},{193,65... | collective-permute-start | bytes 196616 | tf_op jit(solution)/shard_map/ppermute | solution.py:374
  42.7 5.2 %collective-permute-start.10 = (bf16[256,128]{1,0:T(8,128)(2,1)S(1)}, bf16[256,128]{1,0:T(8,128)(2,1)S(1)}, u32[]{:S(2)}, u32[]{:S(2)}) collective-permute-start(bf16[256,128]{1,0:T(8,128)(2,1)S(1)} %get-tuple-element.51), channel_id=1, source_target_pairs={{0,64},{64,128},{128,192},{192,0},{1,65},{65,129},{129,193},{193,1... | collective-permute-start | bytes 196616 | tf_op jit(solution)/shard_map/ppermute | solution.py:374
  48.0 1.6 %collective-permute-start.13 = (bf16[4,256,128]{2,1,0:T(8,128)(2,1)S(1)}, bf16[4,256,128]{2,1,0:T(8,128)(2,1)S(1)}, u32[]{:S(2)}, u32[]{:S(2)}) collective-permute-start(bf16[4,256,128]{2,1,0:T(8,128)(2,1)S(1)} %pad_maximum_fusion.2.hm), channel_id=1, source_target_pairs={{0,1},{1,0},{2,3},{3,2},{4,5},{5,4},{6,7},{7,6},{8,9},{9,8},{10,11... | collective-permute-start | bytes 786440 | tf_op jit(solution)/shard_map/ppermute | solution.py:374
  51.8 13.1 %collective-permute-start.15 = (bf16[512,256]{1,0:T(8,128)(2,1)S(1)}, bf16[512,256]{1,0:T(8,128)(2,1)S(1)}, u32[]{:S(2)}, u32[]{:S(2)}) collective-permute-start(bf16[512,256]{1,0:T(8,128)(2,1)S(1)} %get-tuple-element.58), channel_id=1, source_target_pairs={{0,4},{4,8},{8,12},{12,16},{16,20},{20,24},{24,28},{28,0},{1,5},{5... | collective-permute-start | bytes 786440 | tf_op jit(solution)/shard_map/ppermute | solution.py:374
  54.3 16.2 %collective-permute-start.22 = (bf16[512,256]{1,0:T(8,128)(2,1)S(1)}, bf16[512,256]{1,0:T(8,128)(2,1)S(1)}, u32[]{:S(2)}, u32[]{:S(2)}) collective-permute-start(bf16[512,256]{1,0:T(8,128)(2,1)S(1)} %get-tuple-element.66), channel_id=1, source_target_pairs={{0,4},{4,8},{8,12},{12,16},{16,20},{20,24},{24,28},{28,0},{1,5},{5... | collective-permute-start | bytes 786440 | tf_op jit(solution)/shard_map/ppermute | solution.py:374
  56.3 14.4 %collective-permute-start.18 = (bf16[512,256]{1,0:T(8,128)(2,1)S(1)}, bf16[512,256]{1,0:T(8,128)(2,1)S(1)}, u32[]{:S(2)}, u32[]{:S(2)}) collective-permute-start(bf16[512,256]{1,0:T(8,128)(2,1)S(1)} %get-tuple-element.61), channel_id=1, source_target_pairs={{0,28},{4,0},{8,4},{12,8},{16,12},{20,16},{24,20},{28,24},{1,29},{... | collective-permute-start | bytes 786440 | tf_op jit(solution)/shard_map/ppermute | solution.py:374
  58.4 15.8 %collective-permute-start.26 = (bf16[512,256]{1,0:T(8,128)(2,1)S(1)}, bf16[512,256]{1,0:T(8,128)(2,1)S(1)}, u32[]{:S(2)}, u32[]{:S(2)}) collective-permute-start(bf16[512,256]{1,0:T(8,128)(2,1)S(1)} %get-tuple-element.70), channel_id=1, source_target_pairs={{0,28},{4,0},{8,4},{12,8},{16,12},{20,16},{24,20},{28,24},{1,29},{... | collective-permute-start | bytes 786440 | tf_op jit(solution)/shard_map/ppermute | solution.py:374
  64.9 25.5 %collective-permute-start.16 = (bf16[512,256]{1,0:T(8,128)(2,1)S(1)}, bf16[512,256]{1,0:T(8,128)(2,1)S(1)}, u32[]{:S(2)}, u32[]{:S(2)}) collective-permute-start(bf16[512,256]{1,0:T(8,128)(2,1)S(1)} %add_convert_fusion.10), channel_id=1, source_target_pairs={{0,4},{4,8},{8,12},{12,16},{16,20},{20,24},{24,28},{28,0},{1,5},{5... | collective-permute-start | bytes 786440 | tf_op jit(solution)/shard_map/ppermute | solution.py:374
  70.5 10.6 %collective-permute-start.23 = (bf16[512,256]{1,0:T(8,128)(2,1)S(1)}, bf16[512,256]{1,0:T(8,128)(2,1)S(1)}, u32[]{:S(2)}, u32[]{:S(2)}) collective-permute-start(bf16[512,256]{1,0:T(8,128)(2,1)S(1)} %add_convert_fusion.5), channel_id=1, source_target_pairs={{0,4},{4,8},{8,12},{12,16},{16,20},{20,24},{24,28},{28,0},{1,5},{5... | collective-permute-start | bytes 786440 | tf_op jit(solution)/shard_map/ppermute | solution.py:374
  70.7 10.6 %collective-permute-start.19 = (bf16[512,256]{1,0:T(8,128)(2,1)S(1)}, bf16[512,256]{1,0:T(8,128)(2,1)S(1)}, u32[]{:S(2)}, u32[]{:S(2)}) collective-permute-start(bf16[512,256]{1,0:T(8,128)(2,1)S(1)} %add_convert_fusion.8), channel_id=1, source_target_pairs={{0,28},{4,0},{8,4},{12,8},{16,12},{20,16},{24,20},{28,24},{1,29},{... | collective-permute-start | bytes 786440 | tf_op jit(solution)/shard_map/ppermute | solution.py:374
  74.3 10.5 %collective-permute-start.27 = (bf16[512,256]{1,0:T(8,128)(2,1)S(1)}, bf16[512,256]{1,0:T(8,128)(2,1)S(1)}, u32[]{:S(2)}, u32[]{:S(2)}) collective-permute-start(bf16[512,256]{1,0:T(8,128)(2,1)S(1)} %add_convert_fusion.2), channel_id=1, source_target_pairs={{0,28},{4,0},{8,4},{12,8},{16,12},{20,16},{24,20},{28,24},{1,29},{... | collective-permute-start | bytes 786440 | tf_op jit(solution)/shard_map/ppermute | solution.py:374
  81.2 9.1 %collective-permute-start.24 = (bf16[512,256]{1,0:T(8,128)(2,1)S(1)}, bf16[512,256]{1,0:T(8,128)(2,1)S(1)}, u32[]{:S(2)}, u32[]{:S(2)}) collective-permute-start(bf16[512,256]{1,0:T(8,128)(2,1)S(1)} %add_convert_fusion.4), channel_id=1, source_target_pairs={{0,4},{4,8},{8,12},{12,16},{16,20},{20,24},{24,28},{28,0},{1,5},{5... | collective-permute-start | bytes 786440 | tf_op jit(solution)/shard_map/ppermute | solution.py:374
  81.4 10.1 %collective-permute-start.20 = (bf16[512,256]{1,0:T(8,128)(2,1)S(1)}, bf16[512,256]{1,0:T(8,128)(2,1)S(1)}, u32[]{:S(2)}, u32[]{:S(2)}) collective-permute-start(bf16[512,256]{1,0:T(8,128)(2,1)S(1)} %add_convert_fusion.7), channel_id=1, source_target_pairs={{0,28},{4,0},{8,4},{12,8},{16,12},{20,16},{24,20},{28,24},{1,29},{... | collective-permute-start | bytes 786440 | tf_op jit(solution)/shard_map/ppermute | solution.py:374
  84.7 17.5 %copy-start.4 = (f32[16,256]{1,0:T(8,128)S(1)}, f32[16,256]{1,0:T(8,128)}, u32[]{:S(2)}) copy-start(f32[16,256]{1,0:T(8,128)} %rate_ref.3) | copy-start | bytes 49156
  84.7 17.5 %copy-start.5 = (f32[16,256]{1,0:T(8,128)S(1)}, f32[16,256]{1,0:T(8,128)}, u32[]{:S(2)}) copy-start(f32[16,256]{1,0:T(8,128)} %res_ref.3) | copy-start | bytes 49156
  84.8 12.2 %collective-permute-start.28 = (bf16[512,256]{1,0:T(8,128)(2,1)S(1)}, bf16[512,256]{1,0:T(8,128)(2,1)S(1)}, u32[]{:S(2)}, u32[]{:S(2)}) collective-permute-start(bf16[512,256]{1,0:T(8,128)(2,1)S(1)} %add_convert_fusion.1), channel_id=1, source_target_pairs={{0,28},{4,0},{8,4},{12,8},{16,12},{20,16},{24,20},{28,24},{1,29},{... | collective-permute-start | bytes 786440 | tf_op jit(solution)/shard_map/ppermute | solution.py:374
  90.3 10.5 %collective-permute-start.25 = (bf16[512,256]{1,0:T(8,128)(2,1)S(1)}, bf16[512,256]{1,0:T(8,128)(2,1)S(1)}, u32[]{:S(2)}, u32[]{:S(2)}) collective-permute-start(bf16[512,256]{1,0:T(8,128)(2,1)S(1)} %add_convert_fusion.3), channel_id=1, source_target_pairs={{0,4},{4,8},{8,12},{12,16},{16,20},{20,24},{24,28},{28,0},{1,5},{5... | collective-permute-start | bytes 786440 | tf_op jit(solution)/shard_map/ppermute | solution.py:374
  90.5 13.6 %collective-permute-start.17 = (bf16[512,256]{1,0:T(8,128)(2,1)S(1)}, bf16[512,256]{1,0:T(8,128)(2,1)S(1)}, u32[]{:S(2)}, u32[]{:S(2)}) collective-permute-start(bf16[512,256]{1,0:T(8,128)(2,1)S(1)} %add_convert_fusion.9), channel_id=1, source_target_pairs={{0,4},{4,8},{8,12},{12,16},{16,20},{20,24},{24,28},{28,0},{1,5},{5... | collective-permute-start | bytes 786440 | tf_op jit(solution)/shard_map/ppermute | solution.py:374
  91.5 12.7 %collective-permute-start.21 = (bf16[512,256]{1,0:T(8,128)(2,1)S(1)}, bf16[512,256]{1,0:T(8,128)(2,1)S(1)}, u32[]{:S(2)}, u32[]{:S(2)}) collective-permute-start(bf16[512,256]{1,0:T(8,128)(2,1)S(1)} %add_convert_fusion.6), channel_id=1, source_target_pairs={{0,28},{4,0},{8,4},{12,8},{16,12},{20,16},{24,20},{28,24},{1,29},{... | collective-permute-start | bytes 786440 | tf_op jit(solution)/shard_map/ppermute | solution.py:374
  100.9 8.3 %copy-start.1 = (bf16[512,256]{1,0:T(8,128)(2,1)S(1)}, bf16[512,256]{1,0:T(8,128)(2,1)}, u32[]{:S(2)}) copy-start(bf16[512,256]{1,0:T(8,128)(2,1)} %res.1) | copy-start | bytes 786436
  100.9 8.3 %copy-start.2 = (bf16[512,256]{1,0:T(8,128)(2,1)S(1)}, bf16[512,256]{1,0:T(8,128)(2,1)}, u32[]{:S(2)}) copy-start(bf16[512,256]{1,0:T(8,128)(2,1)} %gate.2) | copy-start | bytes 786436
  100.9 8.2 %copy-start.6 = (f32[3,256]{1,0:T(4,128)S(1)}, f32[3,256]{1,0:T(4,128)}, u32[]{:S(2)}) copy-start(f32[3,256]{1,0:T(4,128)} %taps.3) | copy-start | bytes 9220
  101.0 8.2 %collective-permute-start.29 = (bf16[512,256]{1,0:T(8,128)(2,1)S(1)}, bf16[512,256]{1,0:T(8,128)(2,1)S(1)}, u32[]{:S(2)}, u32[]{:S(2)}) collective-permute-start(bf16[512,256]{1,0:T(8,128)(2,1)S(1)} %add_convert_fusion), channel_id=1, source_target_pairs={{0,2},{2,0},{1,3},{3,1},{4,6},{6,4},{5,7},{7,5},{8,10},{10,8},{9,1... | collective-permute-start | bytes 786440 | tf_op jit(solution)/shard_map/ppermute | solution.py:374
  109.2 10.9 %copy-start.7 = (f32[256]{0:T(256)S(1)}, f32[256]{0:T(256)}, u32[]{:S(2)}) copy-start(f32[256]{0:T(256)} %param.21) | copy-start | bytes 3076
  111.6 3.8 %collective-permute-start.30 = (f32[24,256]{1,0:T(8,128)S(1)}, f32[24,256]{1,0:T(8,128)S(1)}, u32[]{:S(2)}, u32[]{:S(2)}) collective-permute-start(f32[24,256]{1,0:T(8,128)S(1)} %get-tuple-element.78), channel_id=1, source_target_pairs={{0,32},{32,0},{1,33},{33,1},{2,34},{34,2},{3,35},{35,3},{4,36},{36... | collective-permute-start | bytes 73736 | tf_op jit(solution)/shard_map/ppermute | solution.py:374
  115.5 7.0 %collective-permute-start.31 = (f32[2,24,256]{2,1,0:T(8,128)S(1)}, f32[2,24,256]{2,1,0:T(8,128)S(1)}, u32[]{:S(2)}, u32[]{:S(2)}) collective-permute-start(f32[2,24,256]{2,1,0:T(8,128)S(1)} %pad_maximum_fusion.3.g0), channel_id=1, source_target_pairs={{0,64},{64,128},{128,192},{192,0},{1,65},{65,129},{129,193},{193,1... | collective-permute-start | bytes 147464 | tf_op jit(solution)/shard_map/ppermute | solution.py:374
  116.5 6.1 %collective-permute-start.32 = (f32[2,24,256]{2,1,0:T(8,128)S(1)}, f32[2,24,256]{2,1,0:T(8,128)S(1)}, u32[]{:S(2)}, u32[]{:S(2)}) collective-permute-start(f32[2,24,256]{2,1,0:T(8,128)S(1)} %pad_maximum_fusion.3.g0), channel_id=1, source_target_pairs={{0,128},{64,192},{128,0},{192,64},{1,129},{65,193},{129,1},{193,65... | collective-permute-start | bytes 147464 | tf_op jit(solution)/shard_map/ppermute | solution.py:374
  119.5 4.1 %collective-permute-start.33 = (f32[2,24,256]{2,1,0:T(8,128)S(1)}, f32[2,24,256]{2,1,0:T(8,128)S(1)}, u32[]{:S(2)}, u32[]{:S(2)}) collective-permute-start(f32[2,24,256]{2,1,0:T(8,128)S(1)} %pad_maximum_fusion.3.g0), channel_id=1, source_target_pairs={{0,192},{64,0},{128,64},{192,128},{1,193},{65,1},{129,65},{193,129... | collective-permute-start | bytes 147464 | tf_op jit(solution)/shard_map/ppermute | solution.py:374
  120.1 3.5 %copy-start.3 = (bf16[512,256]{1,0:T(8,128)(2,1)S(1)}, bf16[512,256]{1,0:T(8,128)(2,1)}, u32[]{:S(2)}) copy-start(bf16[512,256]{1,0:T(8,128)(2,1)} %gate.3) | copy-start | bytes 786436

commit v2 on v1

--- a/solution.py
+++ b/solution.py
@@ -263,13 +263,15 @@
     filt[...] = total
 
 
-def signal_kernel(own, plus, minus, side, res, gate, taps, rate, in_t, att, sig, blocks, pkg, pad):
+def signal_kernel(
+    own, plus, minus, far_plus, far_minus, far_own, res, gate, taps, rate, in_t, att, sig, blocks, pkg, pad
+):
     rows, width = res.shape
     poles = rate.shape[0]
     f32 = jnp.float32
-    total = (
-        own[...].astype(f32) + plus[...].astype(f32) + minus[...].astype(f32) + side[...].astype(f32)
-    )
+    total = own[...].astype(f32)
+    for piece in (plus, minus, far_plus, far_minus, far_own):
+        total = total + piece[...].astype(f32)
     done = (res[...].astype(f32) + total).astype(jnp.bfloat16)
     att[...] = done
     pad[0:8, :] = jnp.zeros((8, width), f32)
@@ -288,7 +290,7 @@
         sums = [jnp.sum(in_t[n] * piece, axis=0, keepdims=True) for n in range(poles)]
         return span * state + jnp.concatenate(sums, axis=0)
 
-    state = lax.fori_loop(0, rows // BLOCK, step, jnp.zeros((poles, width), f32))
+    state = lax.fori_loop(0, rows // BLOCK, step, jnp.zeros((poles, width), f32), unroll=8)
     pkg[0:poles, :] = state
     pkg[poles : poles + 2, :] = pad[6 + rows : 8 + rows, :]
     pkg[poles + 2 : poles + 4, :] = gate[0:2, :].astype(f32)
@@ -311,7 +313,7 @@
             out[at, cols] = total
         return carry
 
-    lax.fori_loop(0, rows // BLOCK, step, 0)
+    lax.fori_loop(0, rows // BLOCK, step, 0, unroll=2)
 
 
 def finish_kernel(
@@ -363,7 +365,7 @@
         out[at, :] = (gate[at, :].astype(f32) * total).astype(jnp.bfloat16)
         return carry
 
-    lax.fori_loop(0, rows // BLOCK, step, 0)
+    lax.fori_loop(0, rows // BLOCK, step, 0, unroll=8)
 
 
 def tie(value, *others):
@@ -441,21 +443,25 @@
     def join(received, mine):
         return (received.astype(f32) + mine.astype(f32)).astype(bf16)
 
-    def hop(moving, by):
-        return shift(moving, "z", NZ, by)
+    def hop(moving, by, across):
+        if not across:
+            return shift(moving, "z", NZ, by)
+        pairs = [
+            (z * NYH + y, (z + by) % NZ * NYH + 1 - y) for z in range(NZ) for y in range(NYH)
+        ]
+        return lax.ppermute(moving, ("z", "yh"), pairs)
 
     def chain(which, offsets, by):
         moving = part[offsets[0]][which]
         for place, offset in enumerate(offsets):
             if place:
                 moving = join(moving, part[offset][which])
-            moving = hop(moving, by)
+            moving = hop(moving, by, which == 0 and abs(offset) == 1)
         return moving
 
     plus_o = chain(0, [4, 3, 2, 1], 1)
     minus_o = chain(0, [-3, -2, -1], -1)
-    for_other = (part[0][0].astype(f32) + plus_o.astype(f32) + minus_o.astype(f32)).astype(bf16)
-    side = shift(for_other, "yh", NYH, 1)
+    own_o = shift(part[0][0], "yh", NYH, 1)
     minus_p = chain(1, [4, -3, -2, -1], -1)
     plus_p = chain(1, [3, 2, 1], 1)
 
@@ -470,7 +476,7 @@
         4,
         [pltpu.VMEM((rows + 8, width), f32)],
         big=[struct((rows, width), bf16)],
-    )(part[0][1], plus_p, minus_p, side, residual_in, gate_in, short_taps, decay_rates, in_t)
+    )(part[0][1], plus_p, minus_p, plus_o, minus_o, own_o, residual_in, gate_in, short_taps, decay_rates, in_t)
     pair = jnp.stack([package, shift(package, "yl", NYL, 1)])
     pairs = [pair] + [shift(pair, "x", NX, d) for d in range(1, 4)]
     (local,) = local_call(

time: 126 us -> 118 us (0.937)
  waiting for transfers between devices: 57.1 us -> 42.3 us
  starting transfers between devices: 49.9 us -> 56.3 us
    ppermute x30 -> x28, waiting for transfers between devices: 55.7 us -> 35.8 us  [shift(): lax.ppermute(value, axis, [(i, (i + by) % count) for i in range(count)])]
    ppermute x0 -> x2, waiting for transfers between devices: none -> 5.21 us  [hop(): return lax.ppermute(moving, ('z', 'yh'), pairs)]
    ppermute x0 -> x2, starting transfers between devices: none -> 4.62 us  [hop(): return lax.ppermute(moving, ('z', 'yh'), pairs)]
    ppermute x30 -> x28, starting transfers between devices: 43.8 us -> 44.3 us  [shift(): lax.ppermute(value, axis, [(i, (i + by) % count) for i in range(count)])]
where the time goes in v2:
time: 118 us; the launch traced here: 116 us
  starting transfers between devices  56.3 us (48%)
  waiting for transfers between devices  42.3 us (36%)
  Pallas kernels  15.8 us (13%)
    ppermute x28, starting transfers between devices, shift(): lax.ppermute(value, axis, [(i, (i + by) % count) for i in range(count)])  44.3 us
    ppermute x28, waiting for transfers between devices, shift(): lax.ppermute(value, axis, [(i, (i + by) % count) for i in range(count)])  35.8 us
    pallas_call x10, Pallas kernels, call(): pl.pallas_call(kernel, out_shape=out, in_specs=[pl.BlockSpec(memory_space...  15.8 us
    ppermute x4, starting transfers between devices, per_device(): came[a] = lax.ppermute(packed[a], ('x', 'c'), head_route(a))  7.34 us
    ppermute x2, waiting for transfers between devices, hop(): return lax.ppermute(moving, ('z', 'yh'), pairs)  5.21 us
    ppermute x2, starting transfers between devices, hop(): return lax.ppermute(moving, ('z', 'yh'), pairs)  4.62 us
  transfers between devices with their start and end apart: 34, of which 20 were waited for; matrix products, arithmetic and copies ran while one was open for 1% of the time, Pallas kernels for 5%

profile of v2, /device:TPU:26, one launch (start us, length us, event | category | flops | bytes accessed | tf_op | source)
XLA Modules:
  0.0 116.2 jit_solution(1894549047198696457)
XLA Ops:
  0.6 1.3 %shard_map.122 = (bf16[768,128]{1,0:T(8,128)(2,1)S(1)}, bf16[768,128]{1,0:T(8,128)(2,1)S(1)}, bf16[768,128]{1,0:T(8,128)(2,1)S(1)}, bf16[768,128]{1,0:T(8,128)(2,1)S(1)}) custom-call(bf16[512,256]{1,0:T(8,128)(2,1)} %q_ref.1, bf16[512,256]{1,0:T(8,128)(2,1)} %k_ref.1, bf16[512,256]{1,0:T(8,128)(2,1)} %v_ref.1), custom_call_target="tpu_custom_call" | custom-call | flops 2000000000 | bytes 6000000 | tf_op jit(solution)/shard_map/pallas_call | solution.py:38
  1.9 0.1 collective-permute-start.2
  2.0 0.7 collective-permute-start
  2.7 5.1 %collective-permute-start.3 = (bf16[768,128]{1,0:T(8,128)(2,1)S(1)}, bf16[768,128]{1,0:T(8,128)(2,1)S(1)}, u32[]{:S(2)}, u32[]{:S(2)}) collective-permute-start(bf16[768,128]{1,0:T(8,128)(2,1)S(1)} %get-tuple-element.44), channel_id=1, source_target_pairs={{0,65},{1,193},{64,1},{65,129},{128,64},{129,192},{192,0},{193,128... | collective-permute-start | bytes 589832 | tf_op jit(solution)/shard_map/ppermute | solution.py:401
  7.8 1.5 %collective-permute-start.1 = (bf16[768,128]{1,0:T(8,128)(2,1)S(1)}, bf16[768,128]{1,0:T(8,128)(2,1)S(1)}, u32[]{:S(2)}, u32[]{:S(2)}) collective-permute-start(bf16[768,128]{1,0:T(8,128)(2,1)S(1)} %get-tuple-element.42), channel_id=1, source_target_pairs={{0,64},{1,192},{64,0},{65,128},{128,65},{129,193},{192,1},{193,129... | collective-permute-start | bytes 589832 | tf_op jit(solution)/shard_map/ppermute | solution.py:401
  9.3 4.7 %collective-permute-start.5 = (bf16[2,512,128]{2,1,0:T(8,128)(2,1)S(1)}, bf16[2,512,128]{2,1,0:T(8,128)(2,1)S(1)}, u32[]{:S(2)}, u32[]{:S(2)}) collective-permute-start(bf16[2,512,128]{2,1,0:T(8,128)(2,1)S(1)} %pad_maximum_fusion.1.m0), channel_id=1, source_target_pairs={{0,1},{1,0},{2,3},{3,2},{4,5},{5,4},{6,7},{7,6},{8,9},{9,8},{10,11... | collective-permute-start | bytes 786440 | tf_op jit(solution)/shard_map/ppermute | solution.py:376
  14.0 1.2 %collective-permute-done.1.r1 = bf16[768,128]{1,0:T(8,128)(2,1)S(1)} collective-permute-done((bf16[768,128]{1,0:T(8,128)(2,1)S(1)}, bf16[768,128]{1,0:T(8,128)(2,1)S(1)}, u32[]{:S(2)}, u32[]{:S(2)}) %collective-permute-start.1) | collective-permute-done | bytes 196640 | tf_op jit(solution)/shard_map/ppermute | solution.py:401
  15.3 0.7 collective-permute-start.4
  16.0 1.2 collective-permute-done.4.t1
  17.2 2.4 %shard_map.123 = (bf16[4,256,128]{2,1,0:T(8,128)(2,1)S(1)}, f32[4,256,128]{2,1,0:T(8,128)S(1)}, f32[4,256,128]{2,1,0:T(8,128)S(1)}, f32[4,256,128]{2,1,0:T(8,128)S(1)}) custom-call(bf16[768,128]{1,0:T(8,128)(2,1)S(1)} %collective-permute-done.r0, bf16[768,128]{1,0:T(8,128)(2,1)S(1)} %collective-permute-done.1.r1, ...), custom_call_target="tpu_custom_call" | custom-call | flops 4000000000 | bytes 12000000 | tf_op jit(solution)/shard_map/pallas_call | solution.py:38
  19.6 0.6 shard_map.125
  20.2 0.5 collective-permute-start.14
  20.6 0.7 collective-permute-start.7
  21.4 1.3 %collective-permute-start.6 = (bf16[2,512,128]{2,1,0:T(8,128)(2,1)S(1)}, bf16[2,512,128]{2,1,0:T(8,128)(2,1)S(1)}, u32[]{:S(2)}, u32[]{:S(2)}) collective-permute-start(bf16[2,512,128]{2,1,0:T(8,128)(2,1)S(1)} %pad_maximum_fusion.m1), channel_id=1, source_target_pairs={{0,32},{32,0},{1,33},{33,1},{2,34},{34,2},{3,35},{35,3},{4,36},{36... | collective-permute-start | bytes 786440 | tf_op jit(solution)/shard_map/ppermute | solution.py:376
  22.7 7.2 %collective-permute-done.7.m0 = bf16[2,512,128]{2,1,0:T(8,128)(2,1)S(1)} collective-permute-done((bf16[2,512,128]{2,1,0:T(8,128)(2,1)S(1)}, bf16[2,512,128]{2,1,0:T(8,128)(2,1)S(1)}, u32[]{:S(2)}, u32[]{:S(2)}) %collective-permute-start.7) | collective-permute-done | bytes 262176 | tf_op jit(solution)/shard_map/ppermute | solution.py:376
  29.8 4.8 %collective-permute-done.6.m1 = bf16[2,512,128]{2,1,0:T(8,128)(2,1)S(1)} collective-permute-done((bf16[2,512,128]{2,1,0:T(8,128)(2,1)S(1)}, bf16[2,512,128]{2,1,0:T(8,128)(2,1)S(1)}, u32[]{:S(2)}, u32[]{:S(2)}) %collective-permute-start.6) | collective-permute-done | bytes 262176 | tf_op jit(solution)/shard_map/ppermute | solution.py:376
  34.6 1.5 %collective-permute-done.8.t1 = bf16[2,512,128]{2,1,0:T(8,128)(2,1)S(1)} collective-permute-done((bf16[2,512,128]{2,1,0:T(8,128)(2,1)S(1)}, bf16[2,512,128]{2,1,0:T(8,128)(2,1)S(1)}, u32[]{:S(2)}, u32[]{:S(2)}) %collective-permute-start.8) | collective-permute-done | bytes 262176 | tf_op jit(solution)/shard_map/ppermute | solution.py:376
  36.1 2.8 %shard_map.124 = (bf16[256,128]{1,0:T(8,128)(2,1)S(1)}, bf16[256,128]{1,0:T(8,128)(2,1)S(1)}, bf16[256,128]{1,0:T(8,128)(2,1)S(1)}, bf16[256,128]{1,0:T(8,128)(2,1)S(1)}) custom-call(bf16[4,256,128]{2,1,0:T(8,128)(2,1)S(1)} %get-tuple-element.45.q_s, f32[4,256,128]{2,1,0:T(8,128)S(1)} %get-tuple-element.46.acc_ref, ...), custom_call_target="tpu_custom_call" | custom-call | flops 4000000000 | bytes 12000000 | tf_op jit(solution)/shard_map/pallas_call | solution.py:38
  39.0 1.3 %collective-permute-start.10 = (bf16[256,128]{1,0:T(8,128)(2,1)S(1)}, bf16[256,128]{1,0:T(8,128)(2,1)S(1)}, u32[]{:S(2)}, u32[]{:S(2)}) collective-permute-start(bf16[256,128]{1,0:T(8,128)(2,1)S(1)} %get-tuple-element.51), channel_id=1, source_target_pairs={{0,64},{64,128},{128,192},{192,0},{1,65},{65,129},{129,193},{193,1... | collective-permute-start | bytes 196616 | tf_op jit(solution)/shard_map/ppermute | solution.py:376
  40.3 2.6 %collective-permute-start.11 = (bf16[256,128]{1,0:T(8,128)(2,1)S(1)}, bf16[256,128]{1,0:T(8,128)(2,1)S(1)}, u32[]{:S(2)}, u32[]{:S(2)}) collective-permute-start(bf16[256,128]{1,0:T(8,128)(2,1)S(1)} %get-tuple-element.52), channel_id=1, source_target_pairs={{0,128},{64,192},{128,0},{192,64},{1,129},{65,193},{129,1},{193,65... | collective-permute-start | bytes 196616 | tf_op jit(solution)/shard_map/ppermute | solution.py:376
  42.9 0.7 collective-permute-start.12
  43.6 2.8 %collective-permute-done.11 = bf16[256,128]{1,0:T(8,128)(2,1)S(1)} collective-permute-done((bf16[256,128]{1,0:T(8,128)(2,1)S(1)}, bf16[256,128]{1,0:T(8,128)(2,1)S(1)}, u32[]{:S(2)}, u32[]{:S(2)}) %collective-permute-start.11) | collective-permute-done | bytes 65568 | tf_op jit(solution)/shard_map/ppermute | solution.py:376
  46.4 0.8 collective-permute-done.12
  47.2 0.1 collective-permute-start.13
  47.3 1.5 %collective-permute-done.13.ho = bf16[4,256,128]{2,1,0:T(8,128)(2,1)S(1)} collective-permute-done((bf16[4,256,128]{2,1,0:T(8,128)(2,1)S(1)}, bf16[4,256,128]{2,1,0:T(8,128)(2,1)S(1)}, u32[]{:S(2)}, u32[]{:S(2)}) %collective-permute-start.13) | collective-permute-done | bytes 262176 | tf_op jit(solution)/shard_map/ppermute | solution.py:376
  48.9 2.1 %shard_map.126 = (bf16[512,256]{1,0:T(8,128)(2,1)S(1)}, bf16[512,256]{1,0:T(8,128)(2,1)S(1)}, bf16[512,256]{1,0:T(8,128)(2,1)S(1)}, bf16[512,256]{1,0:T(8,128)(2...) custom-call(bf16[4,256,128]{2,1,0:T(8,128)(2,1)S(1)} %pad_maximum_fu, ...), custom_call_target="tpu_custom_call" | custom-call | flops 7000000000 | bytes 21000000 | tf_op jit(solution)/shard_map/pallas_call | solution.py:38
  51.0 5.9 %collective-permute-start.26 = (bf16[512,256]{1,0:T(8,128)(2,1)S(1)}, bf16[512,256]{1,0:T(8,128)(2,1)S(1)}, u32[]{:S(2)}, u32[]{:S(2)}) collective-permute-start(bf16[512,256]{1,0:T(8,128)(2,1)S(1)} %get-tuple-element.69), channel_id=1, source_target_pairs={{0,28},{4,0},{8,4},{12,8},{16,12},{20,16},{24,20},{28,24},{1,29},{... | collective-permute-start | bytes 786440 | tf_op jit(solution)/shard_map/ppermute | solution.py:376
  56.9 0.5 shard_map.127
  57.4 0.1 collective-permute-start.22
  57.5 3.2 %collective-permute-start.18 = (bf16[512,256]{1,0:T(8,128)(2,1)S(1)}, bf16[512,256]{1,0:T(8,128)(2,1)S(1)}, u32[]{:S(2)}, u32[]{:S(2)}) collective-permute-start(bf16[512,256]{1,0:T(8,128)(2,1)S(1)} %get-tuple-element.61), channel_id=1, source_target_pairs={{0,28},{4,0},{8,4},{12,8},{16,12},{20,16},{24,20},{28,24},{1,29},{... | collective-permute-start | bytes 786440 | tf_op jit(solution)/shard_map/ppermute | solution.py:376
  60.7 1.3 %collective-permute-start.29 = (bf16[512,256]{1,0:T(8,128)(2,1)S(1)}, bf16[512,256]{1,0:T(8,128)(2,1)S(1)}, u32[]{:S(2)}, u32[]{:S(2)}) collective-permute-start(bf16[512,256]{1,0:T(8,128)(2,1)S(1)} %get-tuple-element.72), channel_id=1, source_target_pairs={{0,2},{2,0},{1,3},{3,1},{4,6},{6,4},{5,7},{7,5},{8,10},{10,8},{9,1... | collective-permute-start | bytes 786440 | tf_op jit(solution)/shard_map/ppermute | solution.py:376
  62.0 1.6 %collective-permute-done.26 = bf16[512,256]{1,0:T(8,128)(2,1)S(1)} collective-permute-done((bf16[512,256]{1,0:T(8,128)(2,1)S(1)}, bf16[512,256]{1,0:T(8,128)(2,1)S(1)}, u32[]{:S(2)}, u32[]{:S(2)}) %collective-permute-start.26) | collective-permute-done | bytes 262176 | tf_op jit(solution)/shard_map/ppermute | solution.py:376
  63.6 0.1 add_convert_fusion.1
  63.7 3.8 %collective-permute-start.27 = (bf16[512,256]{1,0:T(8,128)(2,1)S(1)}, bf16[512,256]{1,0:T(8,128)(2,1)S(1)}, u32[]{:S(2)}, u32[]{:S(2)}) collective-permute-start(bf16[512,256]{1,0:T(8,128)(2,1)S(1)} %add_convert_fusion.1), channel_id=1, source_target_pairs={{0,28},{4,0},{8,4},{12,8},{16,12},{20,16},{24,20},{28,24},{1,29},{... | collective-permute-start | bytes 786440 | tf_op jit(solution)/shard_map/ppermute | solution.py:376
  67.5 0.4 collective-permute-done.22
  68.0 0.1 collective-permute-start.23
  68.0 1.2 %collective-permute-done.18 = bf16[512,256]{1,0:T(8,128)(2,1)S(1)} collective-permute-done((bf16[512,256]{1,0:T(8,128)(2,1)S(1)}, bf16[512,256]{1,0:T(8,128)(2,1)S(1)}, u32[]{:S(2)}, u32[]{:S(2)}) %collective-permute-start.18) | collective-permute-done | bytes 262176 | tf_op jit(solution)/shard_map/ppermute | solution.py:376
  69.2 0.1 add_convert_fusion.7
  69.3 4.0 %collective-permute-start.19 = (bf16[512,256]{1,0:T(8,128)(2,1)S(1)}, bf16[512,256]{1,0:T(8,128)(2,1)S(1)}, u32[]{:S(2)}, u32[]{:S(2)}) collective-permute-start(bf16[512,256]{1,0:T(8,128)(2,1)S(1)} %add_convert_fusion.7), channel_id=1, source_target_pairs={{0,28},{4,0},{8,4},{12,8},{16,12},{20,16},{24,20},{28,24},{1,29},{... | collective-permute-start | bytes 786440 | tf_op jit(solution)/shard_map/ppermute | solution.py:376
  73.3 0.2 collective-permute-done.15
  73.6 0.1 collective-permute-start.16
  73.7 1.2 %collective-permute-done.27 = bf16[512,256]{1,0:T(8,128)(2,1)S(1)} collective-permute-done((bf16[512,256]{1,0:T(8,128)(2,1)S(1)}, bf16[512,256]{1,0:T(8,128)(2,1)S(1)}, u32[]{:S(2)}, u32[]{:S(2)}) %collective-permute-start.27) | collective-permute-done | bytes 262176 | tf_op jit(solution)/shard_map/ppermute | solution.py:376
  74.9 4.5 %collective-permute-start.28 = (bf16[512,256]{1,0:T(8,128)(2,1)S(1)}, bf16[512,256]{1,0:T(8,128)(2,1)S(1)}, u32[]{:S(2)}, u32[]{:S(2)}) collective-permute-start(bf16[512,256]{1,0:T(8,128)(2,1)S(1)} %add_convert_fusion), channel_id=1, source_target_pairs={{0,30},{2,28},{4,2},{6,0},{8,6},{10,4},{12,10},{14,8},{16,14},{18,... | collective-permute-start | bytes 786440 | tf_op jit(solution)/shard_map/ppermute | solution.py:452
  79.4 0.1 add_convert_fusion.3
  79.5 0.1 collective-permute-start.24
  79.6 0.9 collective-permute-done.19
  80.5 3.8 %collective-permute-start.20 = (bf16[512,256]{1,0:T(8,128)(2,1)S(1)}, bf16[512,256]{1,0:T(8,128)(2,1)S(1)}, u32[]{:S(2)}, u32[]{:S(2)}) collective-permute-start(bf16[512,256]{1,0:T(8,128)(2,1)S(1)} %add_convert_fusion.6), channel_id=1, source_target_pairs={{0,28},{4,0},{8,4},{12,8},{16,12},{20,16},{24,20},{28,24},{1,29},{... | collective-permute-start | bytes 786440 | tf_op jit(solution)/shard_map/ppermute | solution.py:376
  84.3 0.4 collective-permute-done.16
  84.8 0.1 collective-permute-start.17
  84.9 5.5 %collective-permute-done.24 = bf16[512,256]{1,0:T(8,128)(2,1)S(1)} collective-permute-done((bf16[512,256]{1,0:T(8,128)(2,1)S(1)}, bf16[512,256]{1,0:T(8,128)(2,1)S(1)}, u32[]{:S(2)}, u32[]{:S(2)}) %collective-permute-start.24) | collective-permute-done | bytes 262176 | tf_op jit(solution)/shard_map/ppermute | solution.py:376
  90.4 0.2 collective-permute-start.25
  90.6 0.3 collective-permute-done.20
  90.9 0.1 add_convert_fusion.5
  91.0 4.2 %collective-permute-start.21 = (bf16[512,256]{1,0:T(8,128)(2,1)S(1)}, bf16[512,256]{1,0:T(8,128)(2,1)S(1)}, u32[]{:S(2)}, u32[]{:S(2)}) collective-permute-start(bf16[512,256]{1,0:T(8,128)(2,1)S(1)} %add_convert_fusion.5), channel_id=1, source_target_pairs={{0,28},{4,0},{8,4},{12,8},{16,12},{20,16},{24,20},{28,24},{1,29},{... | collective-permute-start | bytes 786440 | tf_op jit(solution)/shard_map/ppermute | solution.py:376
  95.2 0.1 shard_map.128
  95.4 0.6 collective-permute-done.17.plus
  96.0 5.2 %collective-permute-done.25.far_plus = bf16[512,256]{1,0:T(8,128)(2,1)S(1)} collective-permute-done((bf16[512,256]{1,0:T(8,128)(2,1)S(1)}, bf16[512,256]{1,0:T(8,128)(2,1)S(1)}, u32[]{:S(2)}, u32[]{:S(2)}) %collective-permute-start.25) | collective-permute-done | bytes 262176 | tf_op jit(solution)/shard_map/ppermute | solution.py:452
  101.2 2.0 %shard_map.129 = (bf16[512,256]{1,0:T(8,128)(2,1)}, f32[512,256]{1,0:T(8,128)S(1)}, f32[16,16,256]{2,1,0:T(8,128)S(1)}, f32[24,256]{1,0:T(8,128)S(1)}) custom-call(bf16[512,256]{1,0:T(8,128)(2,1)S(1)} %get-tuple-element.57.own, bf16[512,256]{1,0:T(8,128)(2,1)S(1)} %collective-permute-done.17.plus, bf16[512,256]{1,0:T(8,128)(2,1)S(1)} %collective-permute-done.21.minus, ...), custom_call_target="tpu_custom_call" | custom-call | flops 2000000000 | bytes 6000000 | tf_op jit(solution)/shard_map/pallas_call | solution.py:38
  103.2 3.8 %collective-permute-done.30 = f32[24,256]{1,0:T(8,128)S(1)} collective-permute-done((f32[24,256]{1,0:T(8,128)S(1)}, f32[24,256]{1,0:T(8,128)S(1)}, u32[]{:S(2)}, u32[]{:S(2)}) %collective-permute-start.30) | collective-permute-done | bytes 24608 | tf_op jit(solution)/shard_map/ppermute | solution.py:376
  107.0 0.4 collective-permute-start.31
  107.4 2.7 %collective-permute-start.32 = (f32[2,24,256]{2,1,0:T(8,128)S(1)}, f32[2,24,256]{2,1,0:T(8,128)S(1)}, u32[]{:S(2)}, u32[]{:S(2)}) collective-permute-start(f32[2,24,256]{2,1,0:T(8,128)S(1)} %pad_maximum_fusion.3.g0), channel_id=1, source_target_pairs={{0,128},{64,192},{128,0},{192,64},{1,129},{65,193},{129,1},{193,65... | collective-permute-start | bytes 147464 | tf_op jit(solution)/shard_map/ppermute | solution.py:376
  110.1 2.1 %collective-permute-start.33 = (f32[2,24,256]{2,1,0:T(8,128)S(1)}, f32[2,24,256]{2,1,0:T(8,128)S(1)}, u32[]{:S(2)}, u32[]{:S(2)}) collective-permute-start(f32[2,24,256]{2,1,0:T(8,128)S(1)} %pad_maximum_fusion.3.g0), channel_id=1, source_target_pairs={{0,192},{64,0},{128,64},{192,128},{1,193},{65,1},{129,65},{193,129... | collective-permute-start | bytes 147464 | tf_op jit(solution)/shard_map/ppermute | solution.py:376
  112.2 2.3 %shard_map.130.local = f32[512,256]{1,0:T(8,128)S(1)} custom-call(f32[512,256]{1,0:T(8,128)S(1)} %get-tuple-element.75.sig, f32[32,256]{1,0:T(8,128)S(1)} %get-tuple-element.76.filt, f32[1,256]{1,0:T(1,128)S(1)} %bitcast.17), custom_call_target="tpu_custom_call" | custom-call | flops 6000000000 | bytes 18000000 | tf_op jit(solution)/shard_map/pallas_call | solution.py:38
  114.6 1.6 %shard_map.131 = bf16[512,256]{1,0:T(8,128)(2,1)} custom-call(f32[512,256]{1,0:T(8,128)S(1)} %shard_map.130.local, f32[16,16,256]{2,1,0:T(8,128)S(1)} %get-tuple-element.77.blocks, f32[2,24,256]{2,1,0:T(8,128)S(1)} %pad_maximum_fusion.3.g0, f32[2,24,256]{2,1,0:T(8,128)S(1)} %collective-permute-done.31.g1, f32[2,24,256]{2,1,0:T(8,128)S(1)} %collective-permute-done.32.g2, ...), custom_call_target="tpu_custom_call" | custom-call | flops 2000000000 | bytes 6000000 | tf_op jit(solution)/shard_map/pallas_call | solution.py:38
  (48 shorter events, 0.6 us)
Async XLA Ops:
  1.9 7.4 %collective-permute-start.2 = (bf16[768,128]{1,0:T(8,128)(2,1)S(1)}, bf16[768,128]{1,0:T(8,128)(2,1)S(1)}, u32[]{:S(2)}, u32[]{:S(2)}) collective-permute-start(bf16[768,128]{1,0:T(8,128)(2,1)S(1)} %get-tuple-element.43), channel_id=1, source_target_pairs={{0,1},{1,129},{64,65},{65,193},{128,0},{129,128},{192,64},{193,192... | collective-permute-start | bytes 589832 | tf_op jit(solution)/shard_map/ppermute | solution.py:401
  2.0 7.3 %collective-permute-start = (bf16[768,128]{1,0:T(8,128)(2,1)S(1)}, bf16[768,128]{1,0:T(8,128)(2,1)S(1)}, u32[]{:S(2)}, u32[]{:S(2)}) collective-permute-start(bf16[768,128]{1,0:T(8,128)(2,1)S(1)} %get-tuple-element.41), channel_id=1, source_target_pairs={{0,0},{1,128},{64,64},{65,192},{128,1},{129,129},{192,65},{193,193... | collective-permute-start | bytes 589832 | tf_op jit(solution)/shard_map/ppermute | solution.py:401
  2.7 11.3 %collective-permute-start.3 = (bf16[768,128]{1,0:T(8,128)(2,1)S(1)}, bf16[768,128]{1,0:T(8,128)(2,1)S(1)}, u32[]{:S(2)}, u32[]{:S(2)}) collective-permute-start(bf16[768,128]{1,0:T(8,128)(2,1)S(1)} %get-tuple-element.44), channel_id=1, source_target_pairs={{0,65},{1,193},{64,1},{65,129},{128,64},{129,192},{192,0},{193,128... | collective-permute-start | bytes 589832 | tf_op jit(solution)/shard_map/ppermute | solution.py:401
  7.8 7.5 %collective-permute-start.1 = (bf16[768,128]{1,0:T(8,128)(2,1)S(1)}, bf16[768,128]{1,0:T(8,128)(2,1)S(1)}, u32[]{:S(2)}, u32[]{:S(2)}) collective-permute-start(bf16[768,128]{1,0:T(8,128)(2,1)S(1)} %get-tuple-element.42), channel_id=1, source_target_pairs={{0,64},{1,192},{64,0},{65,128},{128,65},{129,193},{192,1},{193,129... | collective-permute-start | bytes 589832 | tf_op jit(solution)/shard_map/ppermute | solution.py:401
  9.3 6.7 %collective-permute-start.5 = (bf16[2,512,128]{2,1,0:T(8,128)(2,1)S(1)}, bf16[2,512,128]{2,1,0:T(8,128)(2,1)S(1)}, u32[]{:S(2)}, u32[]{:S(2)}) collective-permute-start(bf16[2,512,128]{2,1,0:T(8,128)(2,1)S(1)} %pad_maximum_fusion.1.m0), channel_id=1, source_target_pairs={{0,1},{1,0},{2,3},{3,2},{4,5},{5,4},{6,7},{7,6},{8,9},{9,8},{10,11... | collective-permute-start | bytes 786440 | tf_op jit(solution)/shard_map/ppermute | solution.py:376
  15.3 4.3 %copy-start = (bf16[256,8192]{1,0:T(8,128)(2,1)S(1)}, bf16[256,8192]{1,0:T(8,128)(2,1)}, u32[]{:S(2)}) copy-start(bf16[256,8192]{1,0:T(8,128)(2,1)} %w_ref) | copy-start | bytes 12582916
  15.3 1.8 %collective-permute-start.4 = (bf16[2,512,128]{2,1,0:T(8,128)(2,1)S(1)}, bf16[2,512,128]{2,1,0:T(8,128)(2,1)S(1)}, u32[]{:S(2)}, u32[]{:S(2)}) collective-permute-start(bf16[2,512,128]{2,1,0:T(8,128)(2,1)S(1)} %pad_maximum_fusion.m1), channel_id=1, source_target_pairs={{0,1},{1,0},{2,3},{3,2},{4,5},{5,4},{6,7},{7,6},{8,9},{9,8},{10,11... | collective-permute-start | bytes 786440 | tf_op jit(solution)/shard_map/ppermute | solution.py:376
  20.2 28.7 %collective-permute-start.14 = (bf16[16,256,256]{2,1,0:T(8,128)(2,1)S(1)}, bf16[16,256,256]{2,1,0:T(8,128)(2,1)S(1)}, u32[]{:S(2)}, u32[]{:S(2)}) collective-permute-start(bf16[16,256,256]{2,1,0:T(8,128)(2,1)S(1)} %get-tuple-element.56), channel_id=1, source_target_pairs={{0,1},{1,0},{2,3},{3,2},{4,5},{5,4},{6,7},{7,6},{8,9},{9,8},{10,11... | collective-permute-start | bytes 6291464 | tf_op jit(solution)/shard_map/ppermute | solution.py:376
  20.6 9.2 %collective-permute-start.7 = (bf16[2,512,128]{2,1,0:T(8,128)(2,1)S(1)}, bf16[2,512,128]{2,1,0:T(8,128)(2,1)S(1)}, u32[]{:S(2)}, u32[]{:S(2)}) collective-permute-start(bf16[2,512,128]{2,1,0:T(8,128)(2,1)S(1)} %pad_maximum_fusion.1.m0), channel_id=1, source_target_pairs={{0,32},{32,0},{1,33},{33,1},{2,34},{34,2},{3,35},{35,3},{4,36},{36... | collective-permute-start | bytes 786440 | tf_op jit(solution)/shard_map/ppermute | solution.py:376
  21.4 13.2 %collective-permute-start.6 = (bf16[2,512,128]{2,1,0:T(8,128)(2,1)S(1)}, bf16[2,512,128]{2,1,0:T(8,128)(2,1)S(1)}, u32[]{:S(2)}, u32[]{:S(2)}) collective-permute-start(bf16[2,512,128]{2,1,0:T(8,128)(2,1)S(1)} %pad_maximum_fusion.m1), channel_id=1, source_target_pairs={{0,32},{32,0},{1,33},{33,1},{2,34},{34,2},{3,35},{35,3},{4,36},{36... | collective-permute-start | bytes 786440 | tf_op jit(solution)/shard_map/ppermute | solution.py:376
  29.8 4.8 %collective-permute-start.9 = (bf16[2,512,128]{2,1,0:T(8,128)(2,1)S(1)}, bf16[2,512,128]{2,1,0:T(8,128)(2,1)S(1)}, u32[]{:S(2)}, u32[]{:S(2)}) collective-permute-start(bf16[2,512,128]{2,1,0:T(8,128)(2,1)S(1)} %collective-permute-done.7.m0), channel_id=1, source_target_pairs={{0,1},{1,0},{2,3},{3,2},{4,5},{5,4},{6,7},{7,6},{8,9},{9,8},{10,11... | collective-permute-start | bytes 786440 | tf_op jit(solution)/shard_map/ppermute | solution.py:376
  34.6 1.5 %collective-permute-start.8 = (bf16[2,512,128]{2,1,0:T(8,128)(2,1)S(1)}, bf16[2,512,128]{2,1,0:T(8,128)(2,1)S(1)}, u32[]{:S(2)}, u32[]{:S(2)}) collective-permute-start(bf16[2,512,128]{2,1,0:T(8,128)(2,1)S(1)} %collective-permute-done.6.m1), channel_id=1, source_target_pairs={{0,1},{1,0},{2,3},{3,2},{4,5},{5,4},{6,7},{7,6},{8,9},{9,8},{10,11... | collective-permute-start | bytes 786440 | tf_op jit(solution)/shard_map/ppermute | solution.py:376
  39.0 4.7 %collective-permute-start.10 = (bf16[256,128]{1,0:T(8,128)(2,1)S(1)}, bf16[256,128]{1,0:T(8,128)(2,1)S(1)}, u32[]{:S(2)}, u32[]{:S(2)}) collective-permute-start(bf16[256,128]{1,0:T(8,128)(2,1)S(1)} %get-tuple-element.51), channel_id=1, source_target_pairs={{0,64},{64,128},{128,192},{192,0},{1,65},{65,129},{129,193},{193,1... | collective-permute-start | bytes 196616 | tf_op jit(solution)/shard_map/ppermute | solution.py:376
  40.3 6.2 %collective-permute-start.11 = (bf16[256,128]{1,0:T(8,128)(2,1)S(1)}, bf16[256,128]{1,0:T(8,128)(2,1)S(1)}, u32[]{:S(2)}, u32[]{:S(2)}) collective-permute-start(bf16[256,128]{1,0:T(8,128)(2,1)S(1)} %get-tuple-element.52), channel_id=1, source_target_pairs={{0,128},{64,192},{128,0},{192,64},{1,129},{65,193},{129,1},{193,65... | collective-permute-start | bytes 196616 | tf_op jit(solution)/shard_map/ppermute | solution.py:376
  42.9 4.3 %collective-permute-start.12 = (bf16[256,128]{1,0:T(8,128)(2,1)S(1)}, bf16[256,128]{1,0:T(8,128)(2,1)S(1)}, u32[]{:S(2)}, u32[]{:S(2)}) collective-permute-start(bf16[256,128]{1,0:T(8,128)(2,1)S(1)} %get-tuple-element.53), channel_id=1, source_target_pairs={{0,192},{64,0},{128,64},{192,128},{1,193},{65,1},{129,65},{193,129... | collective-permute-start | bytes 196616 | tf_op jit(solution)/shard_map/ppermute | solution.py:376
  47.2 1.6 %collective-permute-start.13 = (bf16[4,256,128]{2,1,0:T(8,128)(2,1)S(1)}, bf16[4,256,128]{2,1,0:T(8,128)(2,1)S(1)}, u32[]{:S(2)}, u32[]{:S(2)}) collective-permute-start(bf16[4,256,128]{2,1,0:T(8,128)(2,1)S(1)} %pad_maximum_fusion.2.hm), channel_id=1, source_target_pairs={{0,1},{1,0},{2,3},{3,2},{4,5},{5,4},{6,7},{7,6},{8,9},{9,8},{10,11... | collective-permute-start | bytes 786440 | tf_op jit(solution)/shard_map/ppermute | solution.py:376
  51.0 12.6 %collective-permute-start.26 = (bf16[512,256]{1,0:T(8,128)(2,1)S(1)}, bf16[512,256]{1,0:T(8,128)(2,1)S(1)}, u32[]{:S(2)}, u32[]{:S(2)}) collective-permute-start(bf16[512,256]{1,0:T(8,128)(2,1)S(1)} %get-tuple-element.69), channel_id=1, source_target_pairs={{0,28},{4,0},{8,4},{12,8},{16,12},{20,16},{24,20},{28,24},{1,29},{... | collective-permute-start | bytes 786440 | tf_op jit(solution)/shard_map/ppermute | solution.py:376
  57.4 10.5 %collective-permute-start.22 = (bf16[512,256]{1,0:T(8,128)(2,1)S(1)}, bf16[512,256]{1,0:T(8,128)(2,1)S(1)}, u32[]{:S(2)}, u32[]{:S(2)}) collective-permute-start(bf16[512,256]{1,0:T(8,128)(2,1)S(1)} %get-tuple-element.65), channel_id=1, source_target_pairs={{0,4},{4,8},{8,12},{12,16},{16,20},{20,24},{24,28},{28,0},{1,5},{5... | collective-permute-start | bytes 786440 | tf_op jit(solution)/shard_map/ppermute | solution.py:376
  57.5 11.7 %collective-permute-start.18 = (bf16[512,256]{1,0:T(8,128)(2,1)S(1)}, bf16[512,256]{1,0:T(8,128)(2,1)S(1)}, u32[]{:S(2)}, u32[]{:S(2)}) collective-permute-start(bf16[512,256]{1,0:T(8,128)(2,1)S(1)} %get-tuple-element.61), channel_id=1, source_target_pairs={{0,28},{4,0},{8,4},{12,8},{16,12},{20,16},{24,20},{28,24},{1,29},{... | collective-permute-start | bytes 786440 | tf_op jit(solution)/shard_map/ppermute | solution.py:376
  60.7 12.8 %collective-permute-start.15 = (bf16[512,256]{1,0:T(8,128)(2,1)S(1)}, bf16[512,256]{1,0:T(8,128)(2,1)S(1)}, u32[]{:S(2)}, u32[]{:S(2)}) collective-permute-start(bf16[512,256]{1,0:T(8,128)(2,1)S(1)} %get-tuple-element.58), channel_id=1, source_target_pairs={{0,4},{4,8},{8,12},{12,16},{16,20},{20,24},{24,28},{28,0},{1,5},{5... | collective-permute-start | bytes 786440 | tf_op jit(solution)/shard_map/ppermute | solution.py:376
  60.7 34.6 %collective-permute-start.29 = (bf16[512,256]{1,0:T(8,128)(2,1)S(1)}, bf16[512,256]{1,0:T(8,128)(2,1)S(1)}, u32[]{:S(2)}, u32[]{:S(2)}) collective-permute-start(bf16[512,256]{1,0:T(8,128)(2,1)S(1)} %get-tuple-element.72), channel_id=1, source_target_pairs={{0,2},{2,0},{1,3},{3,1},{4,6},{6,4},{5,7},{7,5},{8,10},{10,8},{9,1... | collective-permute-start | bytes 786440 | tf_op jit(solution)/shard_map/ppermute | solution.py:376
  63.7 11.2 %collective-permute-start.27 = (bf16[512,256]{1,0:T(8,128)(2,1)S(1)}, bf16[512,256]{1,0:T(8,128)(2,1)S(1)}, u32[]{:S(2)}, u32[]{:S(2)}) collective-permute-start(bf16[512,256]{1,0:T(8,128)(2,1)S(1)} %add_convert_fusion.1), channel_id=1, source_target_pairs={{0,28},{4,0},{8,4},{12,8},{16,12},{20,16},{24,20},{28,24},{1,29},{... | collective-permute-start | bytes 786440 | tf_op jit(solution)/shard_map/ppermute | solution.py:376
  68.0 11.4 %collective-permute-start.23 = (bf16[512,256]{1,0:T(8,128)(2,1)S(1)}, bf16[512,256]{1,0:T(8,128)(2,1)S(1)}, u32[]{:S(2)}, u32[]{:S(2)}) collective-permute-start(bf16[512,256]{1,0:T(8,128)(2,1)S(1)} %add_convert_fusion.4), channel_id=1, source_target_pairs={{0,4},{4,8},{8,12},{12,16},{16,20},{20,24},{24,28},{28,0},{1,5},{5... | collective-permute-start | bytes 786440 | tf_op jit(solution)/shard_map/ppermute | solution.py:376
  69.3 11.2 %collective-permute-start.19 = (bf16[512,256]{1,0:T(8,128)(2,1)S(1)}, bf16[512,256]{1,0:T(8,128)(2,1)S(1)}, u32[]{:S(2)}, u32[]{:S(2)}) collective-permute-start(bf16[512,256]{1,0:T(8,128)(2,1)S(1)} %add_convert_fusion.7), channel_id=1, source_target_pairs={{0,28},{4,0},{8,4},{12,8},{16,12},{20,16},{24,20},{28,24},{1,29},{... | collective-permute-start | bytes 786440 | tf_op jit(solution)/shard_map/ppermute | solution.py:376
  73.6 11.2 %collective-permute-start.16 = (bf16[512,256]{1,0:T(8,128)(2,1)S(1)}, bf16[512,256]{1,0:T(8,128)(2,1)S(1)}, u32[]{:S(2)}, u32[]{:S(2)}) collective-permute-start(bf16[512,256]{1,0:T(8,128)(2,1)S(1)} %add_convert_fusion.9), channel_id=1, source_target_pairs={{0,4},{4,8},{8,12},{12,16},{16,20},{20,24},{24,28},{28,0},{1,5},{5... | collective-permute-start | bytes 786440 | tf_op jit(solution)/shard_map/ppermute | solution.py:376
  74.9 20.3 %copy-start.4 = (f32[16,256]{1,0:T(8,128)S(1)}, f32[16,256]{1,0:T(8,128)}, u32[]{:S(2)}) copy-start(f32[16,256]{1,0:T(8,128)} %rate_ref.3) | copy-start | bytes 49156
  74.9 20.3 %copy-start.5 = (f32[16,256]{1,0:T(8,128)S(1)}, f32[16,256]{1,0:T(8,128)}, u32[]{:S(2)}) copy-start(f32[16,256]{1,0:T(8,128)} %res_ref.3) | copy-start | bytes 49156
  74.9 20.5 %collective-permute-start.28 = (bf16[512,256]{1,0:T(8,128)(2,1)S(1)}, bf16[512,256]{1,0:T(8,128)(2,1)S(1)}, u32[]{:S(2)}, u32[]{:S(2)}) collective-permute-start(bf16[512,256]{1,0:T(8,128)(2,1)S(1)} %add_convert_fusion), channel_id=1, source_target_pairs={{0,30},{2,28},{4,2},{6,0},{8,6},{10,4},{12,10},{14,8},{16,14},{18,... | collective-permute-start | bytes 786440 | tf_op jit(solution)/shard_map/ppermute | solution.py:452
  79.5 10.9 %collective-permute-start.24 = (bf16[512,256]{1,0:T(8,128)(2,1)S(1)}, bf16[512,256]{1,0:T(8,128)(2,1)S(1)}, u32[]{:S(2)}, u32[]{:S(2)}) collective-permute-start(bf16[512,256]{1,0:T(8,128)(2,1)S(1)} %add_convert_fusion.3), channel_id=1, source_target_pairs={{0,4},{4,8},{8,12},{12,16},{16,20},{20,24},{24,28},{28,0},{1,5},{5... | collective-permute-start | bytes 786440 | tf_op jit(solution)/shard_map/ppermute | solution.py:376
  80.5 10.3 %collective-permute-start.20 = (bf16[512,256]{1,0:T(8,128)(2,1)S(1)}, bf16[512,256]{1,0:T(8,128)(2,1)S(1)}, u32[]{:S(2)}, u32[]{:S(2)}) collective-permute-start(bf16[512,256]{1,0:T(8,128)(2,1)S(1)} %add_convert_fusion.6), channel_id=1, source_target_pairs={{0,28},{4,0},{8,4},{12,8},{16,12},{20,16},{24,20},{28,24},{1,29},{... | collective-permute-start | bytes 786440 | tf_op jit(solution)/shard_map/ppermute | solution.py:376
  84.8 11.2 %collective-permute-start.17 = (bf16[512,256]{1,0:T(8,128)(2,1)S(1)}, bf16[512,256]{1,0:T(8,128)(2,1)S(1)}, u32[]{:S(2)}, u32[]{:S(2)}) collective-permute-start(bf16[512,256]{1,0:T(8,128)(2,1)S(1)} %add_convert_fusion.8), channel_id=1, source_target_pairs={{0,4},{4,8},{8,12},{12,16},{16,20},{20,24},{24,28},{28,0},{1,5},{5... | collective-permute-start | bytes 786440 | tf_op jit(solution)/shard_map/ppermute | solution.py:376
  90.4 10.8 %collective-permute-start.25 = (bf16[512,256]{1,0:T(8,128)(2,1)S(1)}, bf16[512,256]{1,0:T(8,128)(2,1)S(1)}, u32[]{:S(2)}, u32[]{:S(2)}) collective-permute-start(bf16[512,256]{1,0:T(8,128)(2,1)S(1)} %add_convert_fusion.2), channel_id=1, source_target_pairs={{0,6},{2,4},{4,10},{6,8},{8,14},{10,12},{12,18},{14,16},{16,22},{1... | collective-permute-start | bytes 786440 | tf_op jit(solution)/shard_map/ppermute | solution.py:452
  91.0 10.2 %copy-start.1 = (bf16[512,256]{1,0:T(8,128)(2,1)S(1)}, bf16[512,256]{1,0:T(8,128)(2,1)}, u32[]{:S(2)}) copy-start(bf16[512,256]{1,0:T(8,128)(2,1)} %res.1) | copy-start | bytes 786436
  91.0 10.2 %copy-start.2 = (bf16[512,256]{1,0:T(8,128)(2,1)S(1)}, bf16[512,256]{1,0:T(8,128)(2,1)}, u32[]{:S(2)}) copy-start(bf16[512,256]{1,0:T(8,128)(2,1)} %gate.2) | copy-start | bytes 786436
  91.0 10.2 %copy-start.6 = (f32[3,256]{1,0:T(4,128)S(1)}, f32[3,256]{1,0:T(4,128)}, u32[]{:S(2)}) copy-start(f32[3,256]{1,0:T(4,128)} %taps.3) | copy-start | bytes 9220
  91.0 10.2 %collective-permute-start.21 = (bf16[512,256]{1,0:T(8,128)(2,1)S(1)}, bf16[512,256]{1,0:T(8,128)(2,1)S(1)}, u32[]{:S(2)}, u32[]{:S(2)}) collective-permute-start(bf16[512,256]{1,0:T(8,128)(2,1)S(1)} %add_convert_fusion.5), channel_id=1, source_target_pairs={{0,28},{4,0},{8,4},{12,8},{16,12},{20,16},{24,20},{28,24},{1,29},{... | collective-permute-start | bytes 786440 | tf_op jit(solution)/shard_map/ppermute | solution.py:376
  101.2 11.0 %copy-start.7 = (f32[256]{0:T(256)S(1)}, f32[256]{0:T(256)}, u32[]{:S(2)}) copy-start(f32[256]{0:T(256)} %param.21) | copy-start | bytes 3076
  103.2 3.8 %collective-permute-start.30 = (f32[24,256]{1,0:T(8,128)S(1)}, f32[24,256]{1,0:T(8,128)S(1)}, u32[]{:S(2)}, u32[]{:S(2)}) collective-permute-start(f32[24,256]{1,0:T(8,128)S(1)} %get-tuple-element.78), channel_id=1, source_target_pairs={{0,32},{32,0},{1,33},{33,1},{2,34},{34,2},{3,35},{35,3},{4,36},{36... | collective-permute-start | bytes 73736 | tf_op jit(solution)/shard_map/ppermute | solution.py:376
  107.0 7.5 %collective-permute-start.31 = (f32[2,24,256]{2,1,0:T(8,128)S(1)}, f32[2,24,256]{2,1,0:T(8,128)S(1)}, u32[]{:S(2)}, u32[]{:S(2)}) collective-permute-start(f32[2,24,256]{2,1,0:T(8,128)S(1)} %pad_maximum_fusion.3.g0), channel_id=1, source_target_pairs={{0,64},{64,128},{128,192},{192,0},{1,65},{65,129},{129,193},{193,1... | collective-permute-start | bytes 147464 | tf_op jit(solution)/shard_map/ppermute | solution.py:376
  107.4 7.1 %collective-permute-start.32 = (f32[2,24,256]{2,1,0:T(8,128)S(1)}, f32[2,24,256]{2,1,0:T(8,128)S(1)}, u32[]{:S(2)}, u32[]{:S(2)}) collective-permute-start(f32[2,24,256]{2,1,0:T(8,128)S(1)} %pad_maximum_fusion.3.g0), channel_id=1, source_target_pairs={{0,128},{64,192},{128,0},{192,64},{1,129},{65,193},{129,1},{193,65... | collective-permute-start | bytes 147464 | tf_op jit(solution)/shard_map/ppermute | solution.py:376
  110.1 4.4 %collective-permute-start.33 = (f32[2,24,256]{2,1,0:T(8,128)S(1)}, f32[2,24,256]{2,1,0:T(8,128)S(1)}, u32[]{:S(2)}, u32[]{:S(2)}) collective-permute-start(f32[2,24,256]{2,1,0:T(8,128)S(1)} %pad_maximum_fusion.3.g0), channel_id=1, source_target_pairs={{0,192},{64,0},{128,64},{192,128},{1,193},{65,1},{129,65},{193,129... | collective-permute-start | bytes 147464 | tf_op jit(solution)/shard_map/ppermute | solution.py:376
  112.2 2.4 %copy-start.3 = (bf16[512,256]{1,0:T(8,128)(2,1)S(1)}, bf16[512,256]{1,0:T(8,128)(2,1)}, u32[]{:S(2)}) copy-start(bf16[512,256]{1,0:T(8,128)(2,1)} %gate.3) | copy-start | bytes 786436
